TPU v7x, 32 devices: a whole 2x2x4 slice. The times are simulated.
32 devices in a mesh: hid: 8 (over z, y), dp: 4 (over x, core).
Axes of the slice: x: 2, y: 2, z: 4, core: 2. Of those that a mesh axis runs over, the one named last changes fastest.
Arguments:
- hidden_acts: bfloat16 [1024, 65536], P('dp', 'hid'), may hold values from -6 to 6
- out_grads: bfloat16 [1024, 1024], P('dp'), may hold values from -6 to 6
- damping: float32 [64], replicated, may hold values from 0.05 to 1
Outputs:
- update: bfloat16 [65536, 1024], P('hid')
All inputs are finite; a program needn't handle non-finite values.
Results may differ from a plain program's by a relative error of at most 0.0023.
Values may be sent and summed in bfloat16 or wider, within the bound.
No kernel may reach another device: no remote copies, remote signals or barrier semaphores. Data moves between devices by JAX's collectives and lax.ppermute only.
A program may use at most 128 MiB of HBM per device.

v0:
```python
import jax
import jax.numpy as jnp
from jax import lax
from jax.sharding import PartitionSpec as P

BLOCK = 1024
ITERS = 3


out_damping = 0.1


def as_sent(value):
    return jax.tree.map(lambda a: a.astype(jnp.bfloat16) if a.dtype == jnp.float32 else a, value)


def partner_2(value, axis, bit):
    mask = 2**bit
    pairs = [(source, source ^ mask) for source in range(lax.axis_size(axis))]
    return lax.ppermute(value, axis, pairs)


def join_block(local_rows):
    row_span = local_rows.shape[1]
    levels = (BLOCK // row_span).bit_length() - 1
    dp_place = lax.axis_index("dp")
    for bit_pos in range(levels):
        partner = jax.tree.map(
            lambda part, own: part.astype(own.dtype),
            partner_2(as_sent(local_rows), "dp", bit_pos),
            local_rows,
        )
        upper = dp_place // 2**bit_pos % 2 == 1
        local_rows = jnp.where(
            upper,
            jnp.concatenate([partner, local_rows], axis=1),
            jnp.concatenate([local_rows, partner], axis=1),
        )
    return local_rows


def spread_rows(local_rows):
    return lax.all_gather(local_rows, ("hid", "dp"), axis=1, tiled=True)


def identity_rows(first_row, row_count, width):
    row_ids = first_row + jnp.arange(row_count, dtype=jnp.int32)
    return (row_ids[:, None] == jnp.arange(width, dtype=jnp.int32)[None, :]).astype(jnp.float32)


def newton_rows(mat_rows, scales, first_row, complete):
    block_count, row_span, matrix_order = mat_rows.shape
    own_ident = identity_rows(first_row, row_span, matrix_order)
    scale_col = scales[:, None, None]
    local_rows = 2.0 * scale_col * own_ident[None] - scale_col * scale_col * mat_rows
    for iteration in range(1, ITERS):
        whole = complete(local_rows)
        product = jnp.einsum("nrk,nkc->nrc", mat_rows, whole, precision=lax.Precision.HIGHEST)
        product = jnp.einsum("nrk,nkc->nrc", product, whole, precision=lax.Precision.HIGHEST)
        own_rows = lax.dynamic_slice_in_dim(whole, first_row, row_span, 1)
        local_rows = 2.0 * own_rows - product
    return local_rows


def local(hidden_acts, out_grads, damping):
    tok_dev, hid_width = hidden_acts.shape
    width = out_grads.shape[1]
    dp_size = lax.axis_size("dp")
    hid_size = lax.axis_size("hid")
    dp_place = lax.axis_index("dp")
    hid_place = lax.axis_index("hid")
    row_count = hid_width // dp_size
    row_span = min(row_count, BLOCK)
    block_count = row_count // row_span
    blocks_hid = hid_width // BLOCK
    token_total = tok_dev * dp_size
    row_start = dp_place * row_count
    first_block = row_start // BLOCK
    offset = row_start % BLOCK
    s_count = width // (hid_size * dp_size)
    s_start = (hid_place * dp_size + dp_place) * s_count
    all_acts, all_grads = (
        lax.all_gather(hidden_acts, "dp", axis=0, tiled=True),
        lax.all_gather(out_grads, "dp", axis=0, tiled=True),
    )
    own_cols = lax.dynamic_slice_in_dim(all_acts, row_start, row_count, 1)
    block_cols = lax.dynamic_slice_in_dim(all_acts, first_block * BLOCK, block_count * BLOCK, 1)
    gram_rows = jnp.einsum(
        "tnr,tnc->nrc",
        own_cols.reshape(token_total, block_count, row_span),
        block_cols.reshape(token_total, block_count, BLOCK),
        preferred_element_type=jnp.float32,
    ).reshape(row_count, BLOCK)
    grad_rows = jnp.einsum("tq,td->qd", own_cols, all_grads, preferred_element_type=jnp.float32)
    grad_own = lax.dynamic_slice_in_dim(all_grads, s_start, s_count, 1)
    s_sum = jnp.einsum("tr,td->rd", grad_own, all_grads, preferred_element_type=jnp.float32)
    block_damping = lax.dynamic_slice_in_dim(
        damping, hid_place * blocks_hid + first_block, block_count
    )
    in_rows = gram_rows.reshape(block_count, row_span, BLOCK) / token_total
    in_rows = in_rows + block_damping[:, None, None] * identity_rows(offset, row_span, BLOCK)[None]
    out_rows = s_sum / token_total + out_damping * identity_rows(s_start, s_count, width)
    block_ssq = jnp.sum(in_rows * in_rows, axis=(1, 2))
    ownership = (
        (first_block + jnp.arange(block_count, dtype=jnp.int32))[:, None]
        == jnp.arange(blocks_hid, dtype=jnp.int32)[None, :]
    ).astype(jnp.float32)
    block_norms = jnp.dot(block_ssq, ownership, precision=lax.Precision.HIGHEST)
    s_ssq = jnp.sum(out_rows * out_rows)
    norm_total, s_total = lax.psum((block_norms, s_ssq), "dp")
    s_total = lax.psum(s_total, "hid")
    block_scales = 1.0 / jnp.sqrt(jnp.dot(ownership, norm_total, precision=lax.Precision.HIGHEST))
    out_scale = (1.0 / jnp.sqrt(s_total)).reshape(1)
    out_local = newton_rows(out_rows[None], out_scale, s_start, spread_rows)
    out_inverse = spread_rows(out_local)[0]
    in_local = newton_rows(in_rows, block_scales, offset, join_block)
    right_rows = jnp.einsum(
        "nrd,de->nre",
        grad_rows.reshape(block_count, row_span, width),
        out_inverse,
        precision=lax.Precision.HIGHEST,
    )
    right_whole = join_block(right_rows)
    update_local = jnp.einsum(
        "nrk,nkd->nrd", in_local, right_whole, precision=lax.Precision.HIGHEST
    )
    update_local = update_local.reshape(row_count, width).astype(jnp.bfloat16)
    return lax.all_gather(update_local, "dp", axis=0, tiled=True)


def solution(mesh):
    return jax.shard_map(
        local,
        mesh=mesh,
        in_specs=(P("dp", "hid"), P("dp", None), P()),
        out_specs=P("hid", None),
        check_vma=False,
    )
```

profile of v0, /device:TPU:0, one launch (start us, length us, event | category | flops | bytes accessed | tf_op | source)
XLA Modules:
  0.0 653.6 jit_solution(460373369429469198)
XLA Ops:
  7.3 6.4 copy.5
  13.9 2.3 fusion.14
  16.2 18.0 %all-gather.11.cloned.1.call-done = bf16[1024,1024]{1,0:T(8,128)(2,1)} async-done(((bf16[256,1024]{1,0:T(8,128)(2,1)}), bf16[1024,1024]{1,0:T(8,128)(2,1)}) %all-gather.11.cloned.1.call-update) | async-done | bytes 2097168 | tf_op jit(solution)/shard_map/all_gather | solution.py:84
  34.2 3.0 multiply_reduce_fusion.1
  37.2 106.7 %all-gather.9.cloned.1.call-done = bf16[1024,8192]{0,1:T(8,128)(2,1)} async-done(((bf16[256,8192]{0,1:T(8,128)(2,1)}), bf16[1024,8192]{0,1:T(8,128)(2,1)}) %all-gather.9.cloned.1.call-update) | async-done | bytes 16777232 | tf_op jit(solution)/shard_map/all_gather | solution.py:83
  143.9 4.6 constant_dynamic-slice_fusion
  148.6 7.1 %multiply_reduce_fusion = (f32[2]{0:T(128)S(1)}, f32[2,1024,1024]{2,1,0:T(8,128)}) fusion(f32[1024,1024]{1,0:T(8,128)S(1)} %copy-done, f32[2]{0:T(128)S(1)} %dynamic_slice.22, bf16[1024,2,1024]{0,2,1:T(8,128)(2,1)S(1)} %bitcast.46, bf16[1024,2,1024]{0,2,1:T(8,128)(2,1)S(1)} %bitcast.47), kind=kOutput, calls=%fused_computation.7 | convolution fusion | flops 4305453056 | bytes 20971536 | tf_op jit(solution)/shard_map/tnr,tnc->nrc/dot_general | solution.py:88
  155.9 6.5 all-reduce
  162.4 22.1 %psum.23 = f32[]{:T(128)} all-reduce(f32[]{:T(128)} %get-tuple-element.5), channel_id=1, replica_groups=mesh['hid'=8,'dp'=4] {'hid'}, use_global_device_ids=true, to_apply=%region_4.5 | all-reduce | flops 1 | bytes 8 | tf_op jit(solution)/shard_map/psum | solution.py:111
  186.1 59.1 %all-gather.17.cloned.1.call-done = f32[1024,1024]{1,0:T(8,128)} async-done(((f32[32,1024]{1,0:T(8,128)}), f32[1024,1024]{1,0:T(8,128)}) %all-gather.17.cloned.1.call-update) | async-done | bytes 4194320 | tf_op jit(solution)/shard_map/all_gather | solution.py:43
  245.1 4.7 fusion.31
  249.8 5.3 convolution_subtract_fusion.1
  255.4 60.4 %all-gather.19.cloned.1.call-done = f32[1024,1024]{1,0:T(8,128)} async-done(((f32[32,1024]{1,0:T(8,128)}), f32[1024,1024]{1,0:T(8,128)}) %all-gather.19.cloned.1.call-update) | async-done | bytes 4194320 | tf_op jit(solution)/shard_map/all_gather | solution.py:43
  315.8 4.7 fusion.32
  320.5 5.3 fusion.18
  326.1 10.9 %fusion.30 = f32[2048,1024]{1,0:T(8,128)} fusion(bf16[1024,2048]{0,1:T(8,128)(2,1)} %copy-done.2, bf16[1024,1024]{1,0:T(8,128)(2,1)} %all-gather.11.cloned.1.call-done), kind=kOutput, calls=%fused_computation.48 | convolution fusion | flops 4294967296 | bytes 14680064 | tf_op jit(solution)/shard_map/tq,td->qd/dot_general | solution.py:94
  337.1 34.0 %fusion.4 = f32[2,1024,1024]{2,1,0:T(8,128)} fusion(f32[2,1024,1024]{2,1,0:T(8,128)} %get-tuple-element.14, f32[2]{0:T(128)S(1)} %get-tuple-element.10, f32[2]{0:T(128)S(1)} %get-tuple-element.9, f32[1024,1024]{1,0:T(8,128)S(1)} %copy-done.1), kind=kOutput, calls=%fused_computation.6 | convolution fusion | flops 25776095232 | bytes 20971536 | tf_op jit(solution)/shard_map/nrk,nkc->nrc/dot_general | solution.py:58
  371.1 34.6 %multiply_subtract_fusion = f32[2,1024,1024]{2,1,0:T(8,128)S(1)} fusion(f32[2,1024,1024]{2,1,0:T(8,128)} %get-tuple-element.14, f32[2,1024,1024]{2,1,0:T(8,128)} %fusion.4, f32[2]{0:T(128)S(1)} %get-tuple-element.10, f32[2]{0:T(128)S(1)} %get-tuple-element.9, f32[1024,1024]{1,0:T(8,128)S(1)} %copy-done.1), kind=kOutput, calls=%fused_computation.3 | convolution fusion | flops 25786580992 | bytes 29360144 | tf_op jit(solution)/shard_map/nrk,nkc->nrc/dot_general | solution.py:59
  405.8 33.0 %fusion.28 = f32[2,1024,1024]{2,1,0:T(8,128)S(1)} fusion(f32[2,1024,1024]{2,1,0:T(8,128)} %get-tuple-element.14, f32[2,1024,1024]{2,1,0:T(8,128)S(1)} %multiply_subtract_fusion), kind=kOutput, calls=%fused_computation.46 | convolution fusion | flops 25769803776 | bytes 25165824 | tf_op jit(solution)/shard_map/nrk,nkc->nrc/dot_general | solution.py:58
  438.8 29.1 %fusion.29 = f32[2,1024,1024]{2,1,0:T(8,128)} fusion(f32[2,1024,1024]{2,1,0:T(8,128)S(1)} %fusion.28, f32[2,1024,1024]{2,1,0:T(8,128)S(1)} %multiply_subtract_fusion), kind=kOutput, calls=%fused_computation.47 | convolution fusion | flops 25769803776 | bytes 25165824 | tf_op jit(solution)/shard_map/nrk,nkc->nrc/dot_general | solution.py:59
  467.9 31.5 %fusion.5 = f32[2,1024,1024]{2,1,0:T(8,128)S(1)} fusion(f32[2,1024,1024]{2,1,0:T(8,128)} %bitcast.48, f32[1,1024,1024]{2,1,0:T(8,128)} %all-gather.13.cloned.1.call-done), kind=kOutput, calls=%fused_computation.9 | convolution fusion | flops 25769803776 | bytes 20971520 | tf_op jit(solution)/shard_map/nrd,de->nre/dot_general | solution.py:117
  499.4 28.4 %fusion.15 = bf16[2,1024,1024]{2,1,0:T(8,128)(2,1)} fusion(f32[2,1024,1024]{2,1,0:T(8,128)S(1)} %fusion.5, f32[2,1024,1024]{2,1,0:T(8,128)S(1)} %copy-done.6, f32[2,1024,1024]{2,1,0:T(8,128)S(1)} %copy-done.5), kind=kOutput, calls=%fused_computation.20 | convolution fusion | flops 25776095232 | bytes 29360128 | tf_op jit(solution)/shard_map/nrk,nkd->nrd/dot_general | solution.py:124
  527.8 104.8 %all-gather.15.cloned.1.call-done = bf16[8192,1024]{1,0:T(8,128)(2,1)} async-done(((bf16[2048,1024]{1,0:T(8,128)(2,1)}), bf16[8192,1024]{1,0:T(8,128)(2,1)}) %all-gather.15.cloned.1.call-update) | async-done | bytes 16777232 | tf_op jit(solution)/shard_map/all_gather | solution.py:128
  632.7 13.9 %copy.9 = bf16[8192,1024]{1,0:T(8,128)(2,1)} copy(bf16[8192,1024]{1,0:T(8,128)(2,1)} %all-gather.15.cloned.1.call-done) | data formatting | bytes 33554432
  (34 shorter events, 2.4 us)
Async XLA Ops:
  6.5 7.3 %copy-start.3 = (f32[64]{0:T(128)S(1)}, f32[64]{0:T(128)}, u32[]{:S(2)}) copy-start(f32[64]{0:T(128)} %param.5) | copy-start | bytes 772
  6.5 27.7 %all-gather.11.cloned.1.call-start = ((), (), s32[]{:S(2)}) async-start(), calls=%async_computation.1 | async-start | bytes 2621440 | tf_op jit(solution)/shard_map/all_gather | solution.py:84
  7.3 136.7 %all-gather.9.cloned.1.call-start = ((), (), s32[]{:S(2)}) async-start(), calls=%async_computation | async-start | bytes 20971520 | tf_op jit(solution)/shard_map/all_gather | solution.py:83
  13.7 231.4 %all-gather.17.cloned.1.call-start = ((), (), s32[]{:S(2)}) async-start(), calls=%async_computation.4 | async-start | bytes 4325376 | tf_op jit(solution)/shard_map/all_gather | solution.py:43
  143.9 4.6 copy-start
  148.6 7.2 %copy-start.2 = (bf16[1024,2048]{0,1:T(8,128)(2,1)}, bf16[1024,2048]{0,1:T(8,128)(2,1)S(1)}, u32[]{:S(2)}) copy-start(bf16[1024,2048]{0,1:T(8,128)(2,1)S(1)} %get-tuple-element.8) | copy-start | bytes 12582916
  186.0 129.8 %all-gather.19.cloned.1.call-start = ((), (), s32[]{:S(2)}) async-start(), calls=%async_computation.5 | async-start | bytes 4325376 | tf_op jit(solution)/shard_map/all_gather | solution.py:43
  255.2 212.7 %all-gather.13.cloned.1.call-start = ((), (), s32[]{:S(2)}) async-start(), calls=%async_computation.2 | async-start | bytes 4325376 | tf_op jit(solution)/shard_map/all_gather | solution.py:43
  325.9 306.8 %all-gather.15.cloned.1.call-start = ((), (), s32[]{:S(2)}) async-start(), calls=%async_computation.3 | async-start | bytes 20971520 | tf_op jit(solution)/shard_map/all_gather | solution.py:128
  326.1 10.9 %copy-start.1 = (f32[1024,1024]{1,0:T(8,128)S(1)}, f32[1024,1024]{1,0:T(8,128)}, u32[]{:S(2)}) copy-start(f32[1024,1024]{1,0:T(8,128)} %fusion.14) | copy-start | bytes 12582916
  405.8 33.0 %copy-start.4 = (f32[2,1024,1024]{2,1,0:T(8,128)}, f32[2,1024,1024]{2,1,0:T(8,128)S(1)}, u32[]{:S(2)}) copy-start(f32[2,1024,1024]{2,1,0:T(8,128)S(1)} %multiply_subtract_fusion) | copy-start | bytes 25165828
  467.9 31.5 %copy-start.5 = (f32[2,1024,1024]{2,1,0:T(8,128)S(1)}, f32[2,1024,1024]{2,1,0:T(8,128)}, u32[]{:S(2)}) copy-start(f32[2,1024,1024]{2,1,0:T(8,128)} %copy-done.4) | copy-start | bytes 25165828
  467.9 31.5 %copy-start.6 = (f32[2,1024,1024]{2,1,0:T(8,128)S(1)}, f32[2,1024,1024]{2,1,0:T(8,128)}, u32[]{:S(2)}) copy-start(f32[2,1024,1024]{2,1,0:T(8,128)} %fusion.29) | copy-start | bytes 25165828
Sparse Core Ops, SparseCore 0:
  8.9 25.2 all-gather.10
  35.8 108.1 all-gather.8
  186.1 58.9 all-gather.16
  255.3 60.4 all-gather.18
  326.0 60.5 all-gather.12
  528.0 104.6 all-gather.14
where the time goes:
time: 661 us; the launch traced here: 654 us
  waiting for transfers between devices  350 us (53%)
  matrix products  232 us (35%)
  blocking collectives  28.7 us (4%)
  local copies, waits for them, and re-layouts  25 us (4%)
  between operations  14.5 us (2%)
    all_gather x3, waiting for transfers between devices, spread_rows(): return lax.all_gather(local_rows, ('hid', 'dp'), axis=1, tiled=True)  119 us
    all_gather x1, waiting for transfers between devices, local(): lax.all_gather(hidden_acts, 'dp', axis=0, tiled=True)  107 us
    all_gather x1, waiting for transfers between devices, local(): return lax.all_gather(update_local, 'dp', axis=0, tiled=True)  105 us
    dot_general x4, matrix products, newton_rows(): jnp.einsum('nrk,nkc->nrc', mat_rows, whole, precision=lax.Precision.HIGHEST)  76.4 us
    dot_general x4, matrix products, newton_rows(): jnp.einsum('nrk,nkc->nrc', product, whole, precision=lax.Precision.HIGHEST)  74.4 us
    dot_general x1, matrix products, local(): jnp.einsum('nrd,de->nre', grad_rows.reshape(block_count, row_span, width)...  31.5 us
    dot_general x1, matrix products, local(): jnp.einsum('nrk,nkd->nrd', in_local, right_whole, precision=lax.Precision...  28.4 us
    psum x1, blocking collectives, local(): s_total = lax.psum(s_total, 'hid')  22.1 us
  transfers between devices with their start and end apart: 6, of which 5 were waited for; matrix products, arithmetic and copies ran while one was open for 24% of the time, Pallas kernels for 0%

commit v1 on v0

v1 whole, which is shorter than its diff:
```python
import functools

import jax
import jax.numpy as jnp
from jax import lax
from jax.experimental import pallas as pl
from jax.experimental.pallas import tpu as pltpu
from jax.sharding import PartitionSpec as P


BLOCK = 1024
ITERS = 3
OUT_DAMPING = 0.1
KERNEL_VMEM = 24 * 2**20
GRAD_CUTS = 4
LATE = 2


ANY = pl.BlockSpec(memory_space=pl.ANY)
VMEM = pl.BlockSpec(memory_space=pltpu.VMEM)
SMEM = pl.BlockSpec(memory_space=pltpu.SMEM)
NN = (((1,), (0,)), ((), ()))
TN = (((0,), (0,)), ((), ()))
TILE = 256


def dot(a, b, dims=NN):
    return lax.dot_general(a, b, dims, preferred_element_type=jnp.float32)


def swap(value, axis, mask):
    pairs = [(source, source ^ mask) for source in range(lax.axis_size(axis))]
    return lax.ppermute(value, axis, pairs)


def aligned(index, size):
    if isinstance(index, int):
        return pl.ds(index * size, size)
    return pl.ds(pl.multiple_of(index * size, size), size)


def gram_tile(pieces, rows, cols):
    value = dot(pieces[0][:, rows], pieces[0][:, cols], TN)
    for piece in pieces[1:]:
        value = value + dot(piece[:, rows], piece[:, cols], TN)
    return value


def upper_gram(pieces, factor):
    for lo in range(0, factor.shape[0], TILE):
        cols, rows = slice(lo, lo + TILE), slice(0, lo + TILE)
        factor[rows, cols] = gram_tile(pieces, rows, cols)


def scaled_factor(pieces, prior, factor, powers, damping, tokens):
    total = jnp.zeros((1, TILE), jnp.float32)
    diagonal = lax.broadcasted_iota(jnp.int32, (TILE, TILE), 0) == lax.broadcasted_iota(
        jnp.int32, (TILE, TILE), 1
    )
    shift = jnp.where(diagonal, damping, 0.0)
    for lo in range(0, factor.shape[0], TILE):
        cols, rows = slice(lo, lo + TILE), slice(0, lo + TILE)
        value = gram_tile(pieces, rows, cols)
        if prior is not None:
            value = value + prior[rows, cols]
        value = value * (1.0 / tokens)
        own = value[lo:] + shift
        factor[cols, cols] = own
        powers[0, cols, cols] = own.astype(jnp.bfloat16)
        total = total + jnp.sum(own * own, axis=0, keepdims=True)
        if lo:
            above = value[:lo]
            factor[:lo, cols] = above
            total = total + 2.0 * jnp.sum(above * above, axis=0, keepdims=True)
            narrow = above.astype(jnp.bfloat16)
            powers[0, :lo, cols] = narrow
            powers[0, cols, :lo] = narrow.T
    return 1.0 / jnp.sqrt(jnp.sum(total, axis=1, keepdims=True))


def residual_powers(factor, scale, powers):
    def square(k, carry):
        first = jnp.where(k == 0, scale, 1.0)
        twice, squared = 2.0 * first, first * first
        for lo in range(0, factor.shape[0], TILE):
            cols, rows = slice(lo, lo + TILE), slice(0, lo + TILE)
            value = twice * factor[rows, cols] - squared * dot(
                powers[k, rows, :], powers[k, :, cols]
            )
            factor[rows, cols] = value
            narrow = value.astype(jnp.bfloat16)
            powers[k + 1, rows, cols] = narrow
            if lo:
                powers[k + 1, cols, :lo] = narrow[:lo].T
        return carry

    lax.fori_loop(0, ITERS - 1, square, 0)


def out_kernel(cuts, tokens, *refs):
    span = tokens // 4
    count = 2 + 2 * cuts
    pieces = refs[:count]
    high_ref, low_ref, grads, factor, powers, wide, sem = refs[count:]
    hid = lax.axis_index("hid")
    small = span // cuts
    starts = [0, span]
    for spot in (2, 3):
        starts += [
            pl.multiple_of(spot * span + lax.rem(hid ^ cut, cuts) * small, small)
            for cut in range(cuts)
        ]
    copies = [
        pltpu.make_async_copy(
            piece, grads.at[pl.ds(start, piece.shape[0])], sem.at[place]
        )
        for place, (piece, start) in enumerate(zip(pieces, starts))
    ]
    start_all(copies)
    wait_all(copies)
    scale = scaled_factor([grads], None, factor, powers, OUT_DAMPING, tokens)
    residual_powers(factor, scale, powers)

    def begin(turn, carry):
        rows = aligned(turn, TILE)
        wide[rows, :] = grads[rows, :].astype(jnp.float32)
        return carry

    lax.fori_loop(0, tokens // TILE, begin, 0)

    def apply(turn, carry):
        last = jnp.where(turn == ITERS - 1, scale, 1.0)
        twice, squared = 2.0 * last, last * last

        def tile(place):
            rows = aligned(place, TILE)
            value = twice * wide[rows, :] - squared * dot(
                grads[rows, :], powers[ITERS - 1 - turn]
            )
            wide[rows, :] = value
            grads[rows, :] = value.astype(jnp.bfloat16)

        in_parts(tokens // TILE, 2, tile)
        return carry

    lax.fori_loop(0, ITERS, apply, 0)

    def finish(turn, carry):
        rows = aligned(turn, TILE)
        high = grads[rows, :]
        high_ref[rows, :] = high
        low_ref[rows, :] = (wide[rows, :] - high.astype(jnp.float32)).astype(jnp.bfloat16)
        return carry

    lax.fori_loop(0, tokens // TILE, finish, 0)


def start_all(copies):
    for copy in copies:
        copy.start()


def wait_all(copies):
    for copy in copies:
        copy.wait()


def precondition_grads(pieces, cuts, tokens):
    width = pieces[0].shape[1]
    return pl.pallas_call(
        functools.partial(out_kernel, cuts, tokens),
        out_shape=[jax.ShapeDtypeStruct((tokens, width), jnp.bfloat16)] * 2,
        in_specs=[VMEM] * len(pieces),
        out_specs=[VMEM] * 2,
        scratch_shapes=[
            pltpu.VMEM((tokens, width), jnp.bfloat16),
            *square_scratch(width),
            pltpu.SemaphoreType.DMA((len(pieces),)),
        ],
        compiler_params=pltpu.CompilerParams(vmem_limit_bytes=KERNEL_VMEM),
        name="out_side",
    )(*pieces)


def square_scratch(width):
    return [
        pltpu.VMEM((BLOCK, BLOCK), jnp.float32),
        pltpu.VMEM((ITERS, BLOCK, BLOCK), jnp.bfloat16),
        pltpu.VMEM((BLOCK, width), jnp.float32),
    ]


def place_copies(source, whole_ref, block, sems, parts=4):
    span = BLOCK // parts
    return [
        pltpu.make_async_copy(
            source.at[pl.ds(part * span, span)],
            whole_ref.at[aligned(block * parts + part, span)],
            sems.at[part],
        )
        for part in range(parts)
    ]


def in_parts(count, parts, body):
    if parts == 1:
        for place in range(count):
            body(place)
        return
    inner = count // parts

    def turn(part, carry):
        for place in range(inner):
            body(part * inner + place)
        return carry

    lax.fori_loop(0, parts, turn, 0)


def right_side(pieces, spots, spread, prior, scale, wide, narrow, parts):
    span = pieces[0].shape[0]

    def tile(place):
        rows = aligned(place, TILE)
        value = prior[rows, :] if prior is not None else None
        for spot, piece in zip(spots, pieces):
            for part in spread:
                term = dot(piece[:, rows], part[spot * span : (spot + 1) * span, :], TN)
                value = term if value is None else value + term
        if scale is not None:
            value = value * scale
        wide[rows, :] = value
        if narrow is not None:
            narrow[rows, :] = value.astype(jnp.bfloat16)

    in_parts(BLOCK // TILE, parts, tile)


def apply_powers(powers, scale, wide, narrow, parts):
    def apply(turn, carry):
        last = jnp.where(turn == ITERS - 1, scale, 1.0)

        def tile(place):
            cols = aligned(place, TILE)
            value = 2.0 * wide[:, cols] - last * dot(
                powers[ITERS - 1 - turn], narrow[:, cols]
            )
            wide[:, cols] = value
            narrow[:, cols] = value.astype(jnp.bfloat16)

        in_parts(wide.shape[1] // TILE, parts, tile)
        return carry

    lax.fori_loop(0, ITERS, apply, 0)


def block_damping(damping_ref, step, blocks):
    return damping_ref[
        lax.axis_index("hid") * blocks + 2 * step + lax.axis_index("dp") % 2
    ]


def moves(places, refs, whole_ref, sem):
    core = lax.axis_index("dp") % 2
    copies = []
    for turn, (own, back) in enumerate(places):
        block = 2 * back + (core if own else 1 - core)
        copies += place_copies(refs[turn], whole_ref, block, sem.at[turn])
    return copies


def block_kernel(parts_at, step, blocks, tokens, spots, places, held, damping_ref, *refs):
    parts = len(spots)
    pieces, spread, refs = refs[:parts], refs[parts : parts + 2], refs[parts + 2 :]
    moving, refs = refs[: len(places)], refs[len(places) + held :]
    whole_ref, send_ref, factor, powers, wide, sem = refs
    copies = moves(places, moving, whole_ref, sem)
    start_all(copies)
    damping = block_damping(damping_ref, step, blocks)
    scale = scaled_factor(pieces, None, factor, powers, damping, tokens)
    residual_powers(factor, scale, powers)
    right_side(pieces, spots, spread, None, scale, wide, send_ref, 2)
    apply_powers(powers, scale, wide, send_ref, parts_at)
    wait_all(copies)


def early_kernel(step, blocks, tokens, spots, places, held, *refs):
    parts = len(spots)
    pieces, spread, refs = refs[:parts], refs[parts : parts + 2], refs[parts + 2 :]
    moving, refs = refs[: len(places)], refs[len(places) + held :]
    whole_ref, gram_ref, right_ref, sem = refs
    copies = moves(places, moving, whole_ref, sem)
    start_all(copies)
    upper_gram(pieces, gram_ref)
    right_side(pieces, spots, spread, None, None, right_ref, None, 2)
    wait_all(copies)


def late_kernel(step, blocks, tokens, spots, places, held, damping_ref, *refs):
    parts = len(spots)
    pieces, spread, refs = refs[:parts], refs[parts : parts + 2], refs[parts + 2 :]
    gram_ref, right_ref, refs = *refs[:2], refs[2:]
    moving, refs = refs[: len(places)], refs[len(places) + held :]
    whole_ref, send_ref, factor, powers, wide, sem = refs
    copies = moves(places, moving, whole_ref, sem)
    start_all(copies)
    damping = block_damping(damping_ref, step, blocks)
    scale = scaled_factor(pieces, gram_ref, factor, powers, damping, tokens)
    residual_powers(factor, scale, powers)
    right_side(pieces, spots, spread, right_ref, scale, wide, send_ref, 2)
    apply_powers(powers, scale, wide, send_ref, 1)
    wait_all(copies)


def call(kernel, operands, specs, outs, out_specs, scratch_shapes, held):
    return pl.pallas_call(
        kernel,
        out_shape=outs,
        in_specs=specs,
        out_specs=out_specs,
        input_output_aliases={len(operands) - 1: 0} if held else {},
        scratch_shapes=scratch_shapes,
        compiler_params=pltpu.CompilerParams(vmem_limit_bytes=KERNEL_VMEM),
    )(*operands)


def block_call(kernel, step, blocks, tokens, damping, pieces, spread, extra, moving, whole):
    width = spread[0].shape[1]
    spots = sorted(pieces)
    held = whole is not None
    operands = [pieces[spot] for spot in spots] + [*spread, *extra, *moving.values()]
    specs = [VMEM] * len(operands)
    if damping is not None:
        operands, specs = [damping] + operands, [SMEM] + specs
    if held:
        operands, specs = operands + [whole], specs + [ANY]
    rows = blocks * BLOCK
    outs = [jax.ShapeDtypeStruct((rows, width), jnp.bfloat16)]
    if damping is None:
        outs.append(jax.ShapeDtypeStruct((BLOCK, BLOCK), jnp.float32))
        outs.append(jax.ShapeDtypeStruct((BLOCK, width), jnp.float32))
        shapes = []
    else:
        outs.append(jax.ShapeDtypeStruct((BLOCK, width), jnp.bfloat16))
        shapes = square_scratch(width)
    shapes = shapes + [pltpu.SemaphoreType.DMA((2, 4))]
    kernel = functools.partial(kernel, step, blocks, tokens, spots, list(moving), held)
    out_specs = [ANY] + [VMEM] * (len(outs) - 1)
    return call(kernel, operands, specs, outs, out_specs, shapes, held)


def place_kernel(step, own, source, held_ref, whole_ref, sem):
    core = lax.axis_index("dp") % 2
    copies = place_copies(source, whole_ref, 2 * step + (core if own else 1 - core), sem, 8)
    start_all(copies)
    wait_all(copies)


def place(step, own, source, whole):
    return call(
        functools.partial(place_kernel, step, own),
        [source, whole],
        [VMEM, ANY],
        jax.ShapeDtypeStruct(whole.shape, whole.dtype),
        ANY,
        [pltpu.SemaphoreType.DMA((8,))],
        True,
    )


def local(cuts, hidden_acts, out_grads, damping):
    span = hidden_acts.shape[0]
    tokens = span * lax.axis_size("dp")
    core = lax.axis_index("dp") % 2
    blocks = hidden_acts.shape[1] // BLOCK
    steps = blocks // 2
    spots = range(1, lax.axis_size("dp"))

    small = span // cuts
    part = lax.dynamic_slice_in_dim(out_grads, lax.axis_index("hid") % cuts * small, small, 0)
    over = [swap(part, "dp", LATE)]
    over += [swap(over[0], "hid", cut) for cut in range(1, cuts)]
    side = swap(out_grads, "dp", 1)
    cross = [swap(over[cut], "dp", 1) for cut in range(cuts)]

    def columns(step, which):
        return lax.dynamic_slice_in_dim(hidden_acts, (2 * step + which) * BLOCK, BLOCK, 1)

    pieces = []
    for step in range(steps):
        same, other = columns(step, core), columns(step, 1 - core)
        pieces.append({0: same})
        for spot in spots:
            pieces[step][spot] = swap(other if spot % 2 else same, "dp", spot)

    spread = precondition_grads([out_grads, side, *over, *cross], cuts, tokens)
    sends, backs = [], []
    whole = None

    def moving(step):
        ready = {}
        if 1 <= step <= len(sends):
            ready[True, step - 1] = sends[step - 1]
        if step >= 2:
            ready[False, step - 2] = backs[step - 2]
        return ready

    for step in range(steps - 1):
        whole, send = block_call(
            functools.partial(block_kernel, 1), step, blocks, tokens, damping, pieces[step], spread, (),
            moving(step), whole,
        )
        sends.append(send)
        backs.append(swap(send, "dp", 1))
    step = steps - 1
    late = {LATE: pieces[step].pop(LATE)}
    whole, gram, right = block_call(
        early_kernel, step, blocks, tokens, None, pieces[step], spread, (),
        moving(step), whole,
    )
    ready = {(False, step - 1): backs[step - 1]} if step else {}
    whole, send = block_call(
        late_kernel, step, blocks, tokens, damping, late, spread, (gram, right),
        ready, whole,
    )
    last = swap(send, "dp", 1)
    whole = place(step, True, send, whole)
    return place(step, False, last, whole)


def solution(mesh):
    hid_size = mesh.shape["hid"]
    cuts = min(GRAD_CUTS, hid_size & -hid_size)

    def body(hidden_acts, out_grads, damping):
        return local(cuts, hidden_acts, out_grads, damping)

    def run(hidden_acts, out_grads, damping):
        step = jax.shard_map(
            body,
            mesh=mesh,
            in_specs=(P("dp", "hid"), P("dp", None), P()),
            out_specs=P("hid", None),
            check_vma=False,
        )
        return step(hidden_acts, out_grads, damping)

    return run
```

time: 661 us -> 167 us (0.25); the launches traced: 654 us -> 167 us
  waiting for transfers between devices: 350 us -> 54.2 us
  matrix products: 232 us -> 0 us
  Pallas kernels: 0 us -> 89.5 us
  blocking collectives: 28.7 us -> 0 us
  local copies, waits for them, and re-layouts: 25 us -> 3.53 us
  starting transfers between devices: 0.42 us -> 19.3 us
  between operations: 14.5 us -> 0.31 us
    all_gather x6 -> x0, waiting for transfers between devices: 349 us -> none  [the longest x3 119 us: spread_rows(): return lax.all_gather(local_rows, ('hid', 'dp'), axis=1, tiled=True)]
    dot_general x15 -> x0, matrix products: 232 us -> none  [the longest x4 76.4 us: newton_rows(): jnp.einsum('nrk,nkc->nrc', mat_rows, whole, precision=lax.Precision.HIGHEST)]
    pallas_call x0 -> x8, Pallas kernels: none -> 89.5 us  [the longest x7 73.4 us: call(): pl.pallas_call(kernel, out_shape=outs, in_specs=specs, out_specs=out_spec...]
    ppermute x0 -> x25, waiting for transfers between devices: none -> 54.2 us  [swap(): return lax.ppermute(value, axis, pairs)]
    psum x2 -> x0, blocking collectives: 28.7 us -> none  [the longest x1 22.1 us: local(): s_total = lax.psum(s_total, 'hid')]
    unnamed x16 -> x4, local copies, waits for them, and re-layouts: 20.3 us -> 0.01 us
    ppermute x0 -> x25, starting transfers between devices: none -> 19.3 us  [swap(): return lax.ppermute(value, axis, pairs)]
  transfers between devices with their start and end apart: 6 -> 25, of which waited for: 5 -> 15; matrix products, arithmetic and copies ran while one was open for 24% -> 2% of each run, Pallas kernels for 0% -> 34%
where the time goes in v1:
time: 167 us
  Pallas kernels  89.5 us (54%)
  waiting for transfers between devices  54.2 us (32%)
  starting transfers between devices  19.3 us (12%)
  local copies, waits for them, and re-layouts  3.53 us (2%)
    pallas_call x7, Pallas kernels, call(): pl.pallas_call(kernel, out_shape=outs, in_specs=specs, out_specs=out_spec...  73.4 us
    ppermute x25, waiting for transfers between devices, swap(): return lax.ppermute(value, axis, pairs)  54.2 us
    ppermute x25, starting transfers between devices, swap(): return lax.ppermute(value, axis, pairs)  19.3 us
    pallas_call x1, Pallas kernels, precondition_grads(): pl.pallas_call(functools.partial(out_kernel, cuts, tokens), out_shape=[ja...  16 us
  transfers between devices with their start and end apart: 25, of which 15 were waited for; matrix products, arithmetic and copies ran while one was open for 2% of the time, Pallas kernels for 34%

profile of v1, /device:TPU:0, one launch (start us, length us, event | category | flops | bytes accessed | tf_op | source)
XLA Modules:
  0.0 166.9 jit_solution(3179344476602195719)
XLA Ops:
  0.9 3.0 %collective-permute-start.2 = (bf16[64,1024]{1,0:T(8,128)(2,1)S(1)}, bf16[64,1024]{1,0:T(8,128)(2,1)S(1)}, u32[]{:S(2)}, u32[]{:S(2)}) collective-permute-start(bf16[64,1024]{1,0:T(8,128)(2,1)S(1)} %constant_dynamic-slice_fusion.7), channel_id=1, source_target_pairs={{0,2},{1,3},{2,0},{3,1},{4,6},{5,7},{6,4},{7,5},{8,10},{9,11},{10,... | collective-permute-start | bytes 393224 | tf_op jit(solution)/shard_map/ppermute | solution.py:33
  4.0 3.5 %collective-permute-done.2.refs_2_ = bf16[64,1024]{1,0:T(8,128)(2,1)S(1)} collective-permute-done((bf16[64,1024]{1,0:T(8,128)(2,1)S(1)}, bf16[64,1024]{1,0:T(8,128)(2,1)S(1)}, u32[]{:S(2)}, u32[]{:S(2)}) %collective-permute-start.2) | collective-permute-done | bytes 131104 | tf_op jit(solution)/shard_map/ppermute | solution.py:33
  7.4 1.8 %collective-permute-start.3 = (bf16[64,1024]{1,0:T(8,128)(2,1)S(1)}, bf16[64,1024]{1,0:T(8,128)(2,1)S(1)}, u32[]{:S(2)}, u32[]{:S(2)}) collective-permute-start(bf16[64,1024]{1,0:T(8,128)(2,1)S(1)} %collective-permute-done.2.refs_2_), channel_id=1, source_target_pairs={{0,4},{4,0},{8,12},{12,8},{16,20},{20,16},{24,28},{28,24},{1,5},{5... | collective-permute-start | bytes 393224 | tf_op jit(solution)/shard_map/ppermute | solution.py:33
  9.2 1.6 collective-permute-start.4
  10.9 2.6 %constant_dynamic-slice_fusion = (bf16[256,1024]{1,0:T(8,128)(2,1)S(1)}, bf16[256,1024]{1,0:T(8,128)(2,1)S(1)}, bf16[256,1024]{1,0:T(8,128)(2,1)S(1)}, bf16[256,...) fusion(bf16[256,8192]{1,0:T(8,128)(2,1)} %param.3, ...), kind=kLoop, calls=%fused_computation | loop fusion | bytes 8388640 | tf_op jit(solution)/shard_map/dynamic_slice | solution.py:387
  14.7 1.5 collective-permute-start.19
  16.7 1.8 %collective-permute-start.7 = (bf16[64,1024]{1,0:T(8,128)(2,1)S(1)}, bf16[64,1024]{1,0:T(8,128)(2,1)S(1)}, u32[]{:S(2)}, u32[]{:S(2)}) collective-permute-start(bf16[64,1024]{1,0:T(8,128)(2,1)S(1)} %collective-permute-done.3.refs_3_), channel_id=1, source_target_pairs={{0,1},{1,0},{2,3},{3,2},{4,5},{5,4},{6,7},{7,6},{8,9},{9,8},{10,11... | collective-permute-start | bytes 393224 | tf_op jit(solution)/shard_map/ppermute | solution.py:33
  22.2 16.0 %out_side.1 = (bf16[1024,1024]{1,0:T(8,128)(2,1)S(1)}, bf16[1024,1024]{1,0:T(8,128)(2,1)S(1)}) custom-call(bf16[256,1024]{1,0:T(8,128)(2,1)S(1)} %copy-done, bf16[256,1024]{1,0:T(8,128)(2,1)S(1)} %collective-permute-done.1.refs_1_, bf16[64,1024]{1,0:T(8,128)(2,1)S(1)} %collective-permute-done.2.refs_2_, bf16[64,1024]{1,0:T(8,128)(2,1)S(1)} %collective-permute-done.3.refs_3_, ...), custom_call_target="tpu_custom_call" | custom-call | tf_op jit(solution)/shard_map/out_side/pallas_call | solution.py:170
  38.5 17.5 %shard_map.37 = (bf16[8192,1024]{1,0:T(8,128)(2,1)}, bf16[1024,1024]{1,0:T(8,128)(2,1)S(1)}) custom-call(f32[64]{0:T(128)S(1)} %copy-done.1, bf16[256,1024]{1,0:T(8,128)(2,1)S(1)} %get-tuple-element.38.refs_0_, bf16[256,1024]{1,0:T(8,128)(2,1)S(1)} %collective-permute-done.18.refs_1_, bf16[256,1024]{1,0:T(8,128)(2,1)S(1)} %collective-permute-done.19.refs_2_, ...), custom_call_target="tpu_custom_call" | custom-call | tf_op jit(solution)/shard_map/pallas_call | solution.py:316
  56.8 1.7 %collective-permute-start.16 = (bf16[256,1024]{1,0:T(8,128)(2,1)S(1)}, bf16[256,1024]{1,0:T(8,128)(2,1)S(1)}, u32[]{:S(2)}, u32[]{:S(2)}) collective-permute-start(bf16[256,1024]{1,0:T(8,128)(2,1)S(1)} %get-tuple-element.33.refs_0_), channel_id=1, source_target_pairs={{0,2},{1,3},{2,0},{3,1},{4,6},{5,7},{6,4},{7,5},{8,10},{9,11},{10,... | collective-permute-start | bytes 1572872 | tf_op jit(solution)/shard_map/ppermute | solution.py:33
  58.9 2.3 %collective-permute-done.15.refs_1_ = bf16[256,1024]{1,0:T(8,128)(2,1)S(1)} collective-permute-done((bf16[256,1024]{1,0:T(8,128)(2,1)S(1)}, bf16[256,1024]{1,0:T(8,128)(2,1)S(1)}, u32[]{:S(2)}, u32[]{:S(2)}) %collective-permute-start.15) | collective-permute-done | bytes 524320 | tf_op jit(solution)/shard_map/ppermute | solution.py:33
  61.2 1.7 %collective-permute-start.13 = (bf16[256,1024]{1,0:T(8,128)(2,1)S(1)}, bf16[256,1024]{1,0:T(8,128)(2,1)S(1)}, u32[]{:S(2)}, u32[]{:S(2)}) collective-permute-start(bf16[256,1024]{1,0:T(8,128)(2,1)S(1)} %get-tuple-element.35.refs_0_), channel_id=1, source_target_pairs={{0,2},{1,3},{2,0},{3,1},{4,6},{5,7},{6,4},{7,5},{8,10},{9,11},{10,... | collective-permute-start | bytes 1572872 | tf_op jit(solution)/shard_map/ppermute | solution.py:33
  63.0 8.6 %collective-permute-done.16.refs_2_ = bf16[256,1024]{1,0:T(8,128)(2,1)S(1)} collective-permute-done((bf16[256,1024]{1,0:T(8,128)(2,1)S(1)}, bf16[256,1024]{1,0:T(8,128)(2,1)S(1)}, u32[]{:S(2)}, u32[]{:S(2)}) %collective-permute-start.16) | collective-permute-done | bytes 524320 | tf_op jit(solution)/shard_map/ppermute | solution.py:33
  71.9 10.1 %collective-permute-done.17.refs_3_ = bf16[256,1024]{1,0:T(8,128)(2,1)S(1)} collective-permute-done((bf16[256,1024]{1,0:T(8,128)(2,1)S(1)}, bf16[256,1024]{1,0:T(8,128)(2,1)S(1)}, u32[]{:S(2)}, u32[]{:S(2)}) %collective-permute-start.17) | collective-permute-done | bytes 524320 | tf_op jit(solution)/shard_map/ppermute | solution.py:33
  82.1 17.3 %shard_map.38 = (bf16[8192,1024]{1,0:T(8,128)(2,1)}, bf16[1024,1024]{1,0:T(8,128)(2,1)S(1)}) custom-call(f32[64]{0:T(128)S(1)} %copy-done.1, bf16[256,1024]{1,0:T(8,128)(2,1)S(1)} %get-tuple-element.33.refs_0_, bf16[256,1024]{1,0:T(8,128)(2,1)S(1)} %collective-permute-done.15.refs_1_, ...), custom_call_target="tpu_custom_call", output_to_operand_aliasing={{0}: (8, {})} | custom-call | tf_op jit(solution)/shard_map/pallas_call | solution.py:316
  100.0 4.1 %collective-permute-done.14.refs_3_ = bf16[256,1024]{1,0:T(8,128)(2,1)S(1)} collective-permute-done((bf16[256,1024]{1,0:T(8,128)(2,1)S(1)}, bf16[256,1024]{1,0:T(8,128)(2,1)S(1)}, u32[]{:S(2)}, u32[]{:S(2)}) %collective-permute-start.14) | collective-permute-done | bytes 524320 | tf_op jit(solution)/shard_map/ppermute | solution.py:33
  104.2 17.6 %shard_map.39 = (bf16[8192,1024]{1,0:T(8,128)(2,1)}, bf16[1024,1024]{1,0:T(8,128)(2,1)S(1)}) custom-call(f32[64]{0:T(128)S(1)} %copy-done.1, bf16[256,1024]{1,0:T(8,128)(2,1)S(1)} %get-tuple-element.35.refs_0_, bf16[256,1024]{1,0:T(8,128)(2,1)S(1)} %collective-permute-done.12.refs_1_, ...), custom_call_target="tpu_custom_call", output_to_operand_aliasing={{0}: (9, {})} | custom-call | tf_op jit(solution)/shard_map/pallas_call | solution.py:316
  122.4 1.7 %collective-permute-start.11 = (bf16[256,1024]{1,0:T(8,128)(2,1)S(1)}, bf16[256,1024]{1,0:T(8,128)(2,1)S(1)}, u32[]{:S(2)}, u32[]{:S(2)}) collective-permute-start(bf16[256,1024]{1,0:T(8,128)(2,1)S(1)} %get-tuple-element.36), channel_id=1, source_target_pairs={{0,3},{1,2},{2,1},{3,0},{4,7},{5,6},{6,5},{7,4},{8,11},{9,10},{10,... | collective-permute-start | bytes 1572872 | tf_op jit(solution)/shard_map/ppermute | solution.py:33
  124.3 2.4 %collective-permute-done.10.refs_1_ = bf16[256,1024]{1,0:T(8,128)(2,1)S(1)} collective-permute-done((bf16[256,1024]{1,0:T(8,128)(2,1)S(1)}, bf16[256,1024]{1,0:T(8,128)(2,1)S(1)}, u32[]{:S(2)}, u32[]{:S(2)}) %collective-permute-start.10) | collective-permute-done | bytes 524320 | tf_op jit(solution)/shard_map/ppermute | solution.py:33
  126.8 9.6 %collective-permute-done.11.refs_2_ = bf16[256,1024]{1,0:T(8,128)(2,1)S(1)} collective-permute-done((bf16[256,1024]{1,0:T(8,128)(2,1)S(1)}, bf16[256,1024]{1,0:T(8,128)(2,1)S(1)}, u32[]{:S(2)}, u32[]{:S(2)}) %collective-permute-start.11) | collective-permute-done | bytes 524320 | tf_op jit(solution)/shard_map/ppermute | solution.py:33
  136.4 5.0 %shard_map.40 = (bf16[8192,1024]{1,0:T(8,128)(2,1)}, f32[1024,1024]{1,0:T(8,128)S(1)}, f32[1024,1024]{1,0:T(8,128)S(1)}) custom-call(bf16[256,1024]{1,0:T(8,128)(2,1)S(1)} %get-tuple-element.37.refs_0_, bf16[256,1024]{1,0:T(8,128)(2,1)S(1)} %collective-permute-done.10.refs_1_, ...), custom_call_target="tpu_custom_call", output_to_operand_aliasing={{0}: (7, {})} | custom-call | tf_op jit(solution)/shard_map/pallas_call | solution.py:316
  141.4 6.5 %collective-permute-done.refs_0_ = bf16[256,1024]{1,0:T(8,128)(2,1)S(1)} collective-permute-done((bf16[256,1024]{1,0:T(8,128)(2,1)S(1)}, bf16[256,1024]{1,0:T(8,128)(2,1)S(1)}, u32[]{:S(2)}, u32[]{:S(2)}) %collective-permute-start) | collective-permute-done | bytes 524320 | tf_op jit(solution)/shard_map/ppermute | solution.py:33
  147.8 13.2 %shard_map.41 = (bf16[8192,1024]{1,0:T(8,128)(2,1)}, bf16[1024,1024]{1,0:T(8,128)(2,1)S(1)}) custom-call(f32[64]{0:T(128)S(1)} %copy-done.1, bf16[256,1024]{1,0:T(8,128)(2,1)S(1)} %collective-permute-done.refs_0_, bf16[1024,1024]{1,0:T(8,128)(2,1)S(1)} %get-tuple-element.18.refs_4_.refs_3_.refs_1_, ...), custom_call_target="tpu_custom_call", output_to_operand_aliasing={{0}: (7, {})} | custom-call | tf_op jit(solution)/shard_map/pallas_call | solution.py:316
  162.6 2.7 %collective-permute-done.24.source = bf16[1024,1024]{1,0:T(8,128)(2,1)S(1)} collective-permute-done((bf16[1024,1024]{1,0:T(8,128)(2,1)S(1)}, bf16[1024,1024]{1,0:T(8,128)(2,1)S(1)}, u32[]{:S(2)}, u32[]{:S(2)}) %collective-permute-start.24) | collective-permute-done | bytes 2097184 | tf_op jit(solution)/shard_map/ppermute | solution.py:33
  (40 shorter events, 12.5 us)
Async XLA Ops:
  0.9 6.5 %collective-permute-start.2 = (bf16[64,1024]{1,0:T(8,128)(2,1)S(1)}, bf16[64,1024]{1,0:T(8,128)(2,1)S(1)}, u32[]{:S(2)}, u32[]{:S(2)}) collective-permute-start(bf16[64,1024]{1,0:T(8,128)(2,1)S(1)} %constant_dynamic-slice_fusion.7), channel_id=1, source_target_pairs={{0,2},{1,3},{2,0},{3,1},{4,6},{5,7},{6,4},{7,5},{8,10},{9,11},{10,... | collective-permute-start | bytes 393224 | tf_op jit(solution)/shard_map/ppermute | solution.py:33
  3.9 18.3 %collective-permute-start.1 = (bf16[256,1024]{1,0:T(8,128)(2,1)}, bf16[256,1024]{1,0:T(8,128)(2,1)S(1)}, u32[]{:S(2)}, u32[]{:S(2)}) collective-permute-start(bf16[256,1024]{1,0:T(8,128)(2,1)} %refs_0_.1), channel_id=1, source_target_pairs={{0,1},{1,0},{2,3},{3,2},{4,5},{5,4},{6,7},{7,6},{8,9},{9,8},{10,11... | collective-permute-start | bytes 1572872 | tf_op jit(solution)/shard_map/ppermute | solution.py:33
  7.4 6.2 %collective-permute-start.3 = (bf16[64,1024]{1,0:T(8,128)(2,1)S(1)}, bf16[64,1024]{1,0:T(8,128)(2,1)S(1)}, u32[]{:S(2)}, u32[]{:S(2)}) collective-permute-start(bf16[64,1024]{1,0:T(8,128)(2,1)S(1)} %collective-permute-done.2.refs_2_), channel_id=1, source_target_pairs={{0,4},{4,0},{8,12},{12,8},{16,20},{20,16},{24,28},{28,24},{1,5},{5... | collective-permute-start | bytes 393224 | tf_op jit(solution)/shard_map/ppermute | solution.py:33
  9.2 5.5 %collective-permute-start.4 = (bf16[64,1024]{1,0:T(8,128)(2,1)S(1)}, bf16[64,1024]{1,0:T(8,128)(2,1)S(1)}, u32[]{:S(2)}, u32[]{:S(2)}) collective-permute-start(bf16[64,1024]{1,0:T(8,128)(2,1)S(1)} %collective-permute-done.2.refs_2_), channel_id=1, source_target_pairs={{0,8},{4,12},{8,0},{12,4},{16,24},{20,28},{24,16},{28,20},{1,9},{5... | collective-permute-start | bytes 393224 | tf_op jit(solution)/shard_map/ppermute | solution.py:33
  10.8 5.9 %collective-permute-start.5 = (bf16[64,1024]{1,0:T(8,128)(2,1)S(1)}, bf16[64,1024]{1,0:T(8,128)(2,1)S(1)}, u32[]{:S(2)}, u32[]{:S(2)}) collective-permute-start(bf16[64,1024]{1,0:T(8,128)(2,1)S(1)} %collective-permute-done.2.refs_2_), channel_id=1, source_target_pairs={{0,12},{4,8},{8,4},{12,0},{16,28},{20,24},{24,20},{28,16},{1,13},{... | collective-permute-start | bytes 393224 | tf_op jit(solution)/shard_map/ppermute | solution.py:33
  13.5 3.1 %collective-permute-start.6 = (bf16[64,1024]{1,0:T(8,128)(2,1)S(1)}, bf16[64,1024]{1,0:T(8,128)(2,1)S(1)}, u32[]{:S(2)}, u32[]{:S(2)}) collective-permute-start(bf16[64,1024]{1,0:T(8,128)(2,1)S(1)} %collective-permute-done.2.refs_2_), channel_id=1, source_target_pairs={{0,1},{1,0},{2,3},{3,2},{4,5},{5,4},{6,7},{7,6},{8,9},{9,8},{10,11... | collective-permute-start | bytes 393224 | tf_op jit(solution)/shard_map/ppermute | solution.py:33
  13.6 24.6 %collective-permute-start.18 = (bf16[256,1024]{1,0:T(8,128)(2,1)S(1)}, bf16[256,1024]{1,0:T(8,128)(2,1)S(1)}, u32[]{:S(2)}, u32[]{:S(2)}) collective-permute-start(bf16[256,1024]{1,0:T(8,128)(2,1)S(1)} %get-tuple-element.31), channel_id=1, source_target_pairs={{0,1},{1,0},{2,3},{3,2},{4,5},{5,4},{6,7},{7,6},{8,9},{9,8},{10,11... | collective-permute-start | bytes 1572872 | tf_op jit(solution)/shard_map/ppermute | solution.py:33
  14.7 23.5 %collective-permute-start.19 = (bf16[256,1024]{1,0:T(8,128)(2,1)S(1)}, bf16[256,1024]{1,0:T(8,128)(2,1)S(1)}, u32[]{:S(2)}, u32[]{:S(2)}) collective-permute-start(bf16[256,1024]{1,0:T(8,128)(2,1)S(1)} %get-tuple-element.38.refs_0_), channel_id=1, source_target_pairs={{0,2},{1,3},{2,0},{3,1},{4,6},{5,7},{6,4},{7,5},{8,10},{9,11},{10,... | collective-permute-start | bytes 1572872 | tf_op jit(solution)/shard_map/ppermute | solution.py:33
  16.7 21.8 %collective-permute-start.20 = (bf16[256,1024]{1,0:T(8,128)(2,1)S(1)}, bf16[256,1024]{1,0:T(8,128)(2,1)S(1)}, u32[]{:S(2)}, u32[]{:S(2)}) collective-permute-start(bf16[256,1024]{1,0:T(8,128)(2,1)S(1)} %get-tuple-element.31), channel_id=1, source_target_pairs={{0,3},{1,2},{2,1},{3,0},{4,7},{5,6},{6,5},{7,4},{8,11},{9,10},{10,... | collective-permute-start | bytes 1572872 | tf_op jit(solution)/shard_map/ppermute | solution.py:33
  16.7 2.8 %collective-permute-start.7 = (bf16[64,1024]{1,0:T(8,128)(2,1)S(1)}, bf16[64,1024]{1,0:T(8,128)(2,1)S(1)}, u32[]{:S(2)}, u32[]{:S(2)}) collective-permute-start(bf16[64,1024]{1,0:T(8,128)(2,1)S(1)} %collective-permute-done.3.refs_3_), channel_id=1, source_target_pairs={{0,1},{1,0},{2,3},{3,2},{4,5},{5,4},{6,7},{7,6},{8,9},{9,8},{10,11... | collective-permute-start | bytes 393224 | tf_op jit(solution)/shard_map/ppermute | solution.py:33
  19.5 1.3 collective-permute-start.8
  56.1 48.1 %collective-permute-start.21 = (bf16[1024,1024]{1,0:T(8,128)(2,1)S(1)}, bf16[1024,1024]{1,0:T(8,128)(2,1)S(1)}, u32[]{:S(2)}, u32[]{:S(2)}) collective-permute-start(bf16[1024,1024]{1,0:T(8,128)(2,1)S(1)} %get-tuple-element.20.refs_6_), channel_id=1, source_target_pairs={{0,1},{1,0},{2,3},{3,2},{4,5},{5,4},{6,7},{7,6},{8,9},{9,8},{10,11... | collective-permute-start | bytes 6291464 | tf_op jit(solution)/shard_map/ppermute | solution.py:33
  56.7 4.5 %collective-permute-start.15 = (bf16[256,1024]{1,0:T(8,128)(2,1)S(1)}, bf16[256,1024]{1,0:T(8,128)(2,1)S(1)}, u32[]{:S(2)}, u32[]{:S(2)}) collective-permute-start(bf16[256,1024]{1,0:T(8,128)(2,1)S(1)} %get-tuple-element.32), channel_id=1, source_target_pairs={{0,1},{1,0},{2,3},{3,2},{4,5},{5,4},{6,7},{7,6},{8,9},{9,8},{10,11... | collective-permute-start | bytes 1572872 | tf_op jit(solution)/shard_map/ppermute | solution.py:33
  56.8 14.8 %collective-permute-start.16 = (bf16[256,1024]{1,0:T(8,128)(2,1)S(1)}, bf16[256,1024]{1,0:T(8,128)(2,1)S(1)}, u32[]{:S(2)}, u32[]{:S(2)}) collective-permute-start(bf16[256,1024]{1,0:T(8,128)(2,1)S(1)} %get-tuple-element.33.refs_0_), channel_id=1, source_target_pairs={{0,2},{1,3},{2,0},{3,1},{4,6},{5,7},{6,4},{7,5},{8,10},{9,11},{10,... | collective-permute-start | bytes 1572872 | tf_op jit(solution)/shard_map/ppermute | solution.py:33
  58.5 23.6 %collective-permute-start.17 = (bf16[256,1024]{1,0:T(8,128)(2,1)S(1)}, bf16[256,1024]{1,0:T(8,128)(2,1)S(1)}, u32[]{:S(2)}, u32[]{:S(2)}) collective-permute-start(bf16[256,1024]{1,0:T(8,128)(2,1)S(1)} %get-tuple-element.32), channel_id=1, source_target_pairs={{0,3},{1,2},{2,1},{3,0},{4,7},{5,6},{6,5},{7,4},{8,11},{9,10},{10,... | collective-permute-start | bytes 1572872 | tf_op jit(solution)/shard_map/ppermute | solution.py:33
  58.5 41.5 %collective-permute-start.12 = (bf16[256,1024]{1,0:T(8,128)(2,1)S(1)}, bf16[256,1024]{1,0:T(8,128)(2,1)S(1)}, u32[]{:S(2)}, u32[]{:S(2)}) collective-permute-start(bf16[256,1024]{1,0:T(8,128)(2,1)S(1)} %get-tuple-element.34), channel_id=1, source_target_pairs={{0,1},{1,0},{2,3},{3,2},{4,5},{5,4},{6,7},{7,6},{8,9},{9,8},{10,11... | collective-permute-start | bytes 1572872 | tf_op jit(solution)/shard_map/ppermute | solution.py:33
  61.2 38.8 %collective-permute-start.13 = (bf16[256,1024]{1,0:T(8,128)(2,1)S(1)}, bf16[256,1024]{1,0:T(8,128)(2,1)S(1)}, u32[]{:S(2)}, u32[]{:S(2)}) collective-permute-start(bf16[256,1024]{1,0:T(8,128)(2,1)S(1)} %get-tuple-element.35.refs_0_), channel_id=1, source_target_pairs={{0,2},{1,3},{2,0},{3,1},{4,6},{5,7},{6,4},{7,5},{8,10},{9,11},{10,... | collective-permute-start | bytes 1572872 | tf_op jit(solution)/shard_map/ppermute | solution.py:33
  71.6 32.6 %collective-permute-start.14 = (bf16[256,1024]{1,0:T(8,128)(2,1)S(1)}, bf16[256,1024]{1,0:T(8,128)(2,1)S(1)}, u32[]{:S(2)}, u32[]{:S(2)}) collective-permute-start(bf16[256,1024]{1,0:T(8,128)(2,1)S(1)} %get-tuple-element.34), channel_id=1, source_target_pairs={{0,3},{1,2},{2,1},{3,0},{4,7},{5,6},{6,5},{7,4},{8,11},{9,10},{10,... | collective-permute-start | bytes 1572872 | tf_op jit(solution)/shard_map/ppermute | solution.py:33
  99.4 37.0 %collective-permute-start.22 = (bf16[1024,1024]{1,0:T(8,128)(2,1)S(1)}, bf16[1024,1024]{1,0:T(8,128)(2,1)S(1)}, u32[]{:S(2)}, u32[]{:S(2)}) collective-permute-start(bf16[1024,1024]{1,0:T(8,128)(2,1)S(1)} %get-tuple-element.22.refs_6_), channel_id=1, source_target_pairs={{0,1},{1,0},{2,3},{3,2},{4,5},{5,4},{6,7},{7,6},{8,9},{9,8},{10,11... | collective-permute-start | bytes 6291464 | tf_op jit(solution)/shard_map/ppermute | solution.py:33
  121.8 26.0 %collective-permute-start.23 = (bf16[1024,1024]{1,0:T(8,128)(2,1)S(1)}, bf16[1024,1024]{1,0:T(8,128)(2,1)S(1)}, u32[]{:S(2)}, u32[]{:S(2)}) collective-permute-start(bf16[1024,1024]{1,0:T(8,128)(2,1)S(1)} %get-tuple-element.24.refs_5_), channel_id=1, source_target_pairs={{0,1},{1,0},{2,3},{3,2},{4,5},{5,4},{6,7},{7,6},{8,9},{9,8},{10,11... | collective-permute-start | bytes 6291464 | tf_op jit(solution)/shard_map/ppermute | solution.py:33
  122.2 4.6 %collective-permute-start.10 = (bf16[256,1024]{1,0:T(8,128)(2,1)S(1)}, bf16[256,1024]{1,0:T(8,128)(2,1)S(1)}, u32[]{:S(2)}, u32[]{:S(2)}) collective-permute-start(bf16[256,1024]{1,0:T(8,128)(2,1)S(1)} %get-tuple-element.36), channel_id=1, source_target_pairs={{0,1},{1,0},{2,3},{3,2},{4,5},{5,4},{6,7},{7,6},{8,9},{9,8},{10,11... | collective-permute-start | bytes 1572872 | tf_op jit(solution)/shard_map/ppermute | solution.py:33
  122.4 14.0 %collective-permute-start.11 = (bf16[256,1024]{1,0:T(8,128)(2,1)S(1)}, bf16[256,1024]{1,0:T(8,128)(2,1)S(1)}, u32[]{:S(2)}, u32[]{:S(2)}) collective-permute-start(bf16[256,1024]{1,0:T(8,128)(2,1)S(1)} %get-tuple-element.36), channel_id=1, source_target_pairs={{0,3},{1,2},{2,1},{3,0},{4,7},{5,6},{6,5},{7,4},{8,11},{9,10},{10,... | collective-permute-start | bytes 1572872 | tf_op jit(solution)/shard_map/ppermute | solution.py:33
  124.0 23.8 %collective-permute-start = (bf16[256,1024]{1,0:T(8,128)(2,1)S(1)}, bf16[256,1024]{1,0:T(8,128)(2,1)S(1)}, u32[]{:S(2)}, u32[]{:S(2)}) collective-permute-start(bf16[256,1024]{1,0:T(8,128)(2,1)S(1)} %get-tuple-element.37.refs_0_), channel_id=1, source_target_pairs={{0,2},{1,3},{2,0},{3,1},{4,6},{5,7},{6,4},{7,5},{8,10},{9,11},{10,... | collective-permute-start | bytes 1572872 | tf_op jit(solution)/shard_map/ppermute | solution.py:33
  161.1 4.2 %collective-permute-start.24 = (bf16[1024,1024]{1,0:T(8,128)(2,1)S(1)}, bf16[1024,1024]{1,0:T(8,128)(2,1)S(1)}, u32[]{:S(2)}, u32[]{:S(2)}) collective-permute-start(bf16[1024,1024]{1,0:T(8,128)(2,1)S(1)} %get-tuple-element.29.source), channel_id=1, source_target_pairs={{0,1},{1,0},{2,3},{3,2},{4,5},{5,4},{6,7},{7,6},{8,9},{9,8},{10,11... | collective-permute-start | bytes 6291464 | tf_op jit(solution)/shard_map/ppermute | solution.py:33
  (3 other events, 54.2 us)

commit v2 on v1

--- a/solution.py
+++ b/solution.py
@@ -22,6 +22,8 @@
 NN = (((1,), (0,)), ((), ()))
 TN = (((0,), (0,)), ((), ()))
 TILE = 256
+PLACE_PARTS = 4
+SOLO_CUTS = (3 * BLOCK // 4, BLOCK // 4)
 
 
 def dot(a, b, dims=NN):
@@ -101,7 +103,7 @@
     span = tokens // 4
     count = 2 + 2 * cuts
     pieces = refs[:count]
-    high_ref, low_ref, grads, factor, powers, wide, sem = refs[count:]
+    grads, powers, scale_ref, factor, sem = refs[count:]
     hid = lax.axis_index("hid")
     small = span // cuts
     starts = [0, span]
@@ -119,11 +121,21 @@
     start_all(copies)
     wait_all(copies)
     scale = scaled_factor([grads], None, factor, powers, OUT_DAMPING, tokens)
+    scale_ref[...] = jnp.broadcast_to(scale, scale_ref.shape)
     residual_powers(factor, scale, powers)
+
+
+def spread_kernel(tokens, given, powers, scale_ref, *refs):
+    high_ref, low_ref, high_half, low_half, grads, wide = refs
+    scale = scale_ref[:1, :1]
+    left = lax.axis_index("dp") % 2 == 0
+    half = wide.shape[1] // 2
 
     def begin(turn, carry):
         rows = aligned(turn, TILE)
-        wide[rows, :] = grads[rows, :].astype(jnp.float32)
+        value = given[rows, :]
+        grads[rows, :] = value
+        wide[rows, :] = value.astype(jnp.float32)
         return carry
 
     lax.fori_loop(0, tokens // TILE, begin, 0)
@@ -140,7 +152,7 @@
             wide[rows, :] = value
             grads[rows, :] = value.astype(jnp.bfloat16)
 
-        in_parts(tokens // TILE, 2, tile)
+        in_parts(tokens // TILE, 1, tile)
         return carry
 
     lax.fori_loop(0, ITERS, apply, 0)
@@ -148,8 +160,11 @@
     def finish(turn, carry):
         rows = aligned(turn, TILE)
         high = grads[rows, :]
+        low = (wide[rows, :] - high.astype(jnp.float32)).astype(jnp.bfloat16)
         high_ref[rows, :] = high
-        low_ref[rows, :] = (wide[rows, :] - high.astype(jnp.float32)).astype(jnp.bfloat16)
+        low_ref[rows, :] = low
+        high_half[rows, :] = jnp.where(left, high[:, :half], high[:, half:])
+        low_half[rows, :] = jnp.where(left, low[:, :half], low[:, half:])
         return carry
 
     lax.fori_loop(0, tokens // TILE, finish, 0)
@@ -165,21 +180,41 @@
         copy.wait()
 
 
-def precondition_grads(pieces, cuts, tokens):
+def out_factor_powers(pieces, cuts, tokens):
     width = pieces[0].shape[1]
     return pl.pallas_call(
         functools.partial(out_kernel, cuts, tokens),
-        out_shape=[jax.ShapeDtypeStruct((tokens, width), jnp.bfloat16)] * 2,
+        out_shape=[
+            jax.ShapeDtypeStruct((tokens, width), jnp.bfloat16),
+            jax.ShapeDtypeStruct((ITERS, width, width), jnp.bfloat16),
+            jax.ShapeDtypeStruct((8, 128), jnp.float32),
+        ],
         in_specs=[VMEM] * len(pieces),
-        out_specs=[VMEM] * 2,
+        out_specs=[VMEM] * 3,
         scratch_shapes=[
-            pltpu.VMEM((tokens, width), jnp.bfloat16),
-            *square_scratch(width),
+            pltpu.VMEM((width, width), jnp.float32),
             pltpu.SemaphoreType.DMA((len(pieces),)),
         ],
         compiler_params=pltpu.CompilerParams(vmem_limit_bytes=KERNEL_VMEM),
-        name="out_side",
+        name="out_factor",
     )(*pieces)
+
+
+def precondition_grads(grads, powers, scale):
+    tokens, width = grads.shape
+    return pl.pallas_call(
+        functools.partial(spread_kernel, tokens),
+        out_shape=[jax.ShapeDtypeStruct((tokens, width), jnp.bfloat16)] * 2
+        + [jax.ShapeDtypeStruct((tokens, width // 2), jnp.bfloat16)] * 2,
+        in_specs=[VMEM] * 3,
+        out_specs=[VMEM] * 4,
+        scratch_shapes=[
+            pltpu.VMEM((tokens, width), jnp.bfloat16),
+            pltpu.VMEM((tokens, width), jnp.float32),
+        ],
+        compiler_params=pltpu.CompilerParams(vmem_limit_bytes=KERNEL_VMEM),
+        name="out_spread",
+    )(grads, powers, scale)
 
 
 def square_scratch(width):
@@ -190,16 +225,33 @@
     ]
 
 
-def place_copies(source, whole_ref, block, sems, parts=4):
-    span = BLOCK // parts
-    return [
-        pltpu.make_async_copy(
-            source.at[pl.ds(part * span, span)],
-            whole_ref.at[aligned(block * parts + part, span)],
-            sems.at[part],
-        )
-        for part in range(parts)
-    ]
+def place_copies(places, refs, whole_ref, sem):
+    core = lax.axis_index("dp") % 2
+    chip = lax.axis_index("dp") // 2 % 2
+    copies = []
+    for (kind, first, second, *rest), ref in zip(places, refs):
+        if kind == "full":
+            block = 2 * second + (core if first else 1 - core)
+            pieces, base, columns = PLACE_PARTS, 0, slice(None)
+        else:
+            block = whole_ref.shape[0] // BLOCK - 2 + (chip if first else 1 - chip)
+            pieces, base = 1, rest[0]
+            columns = aligned(core if second else 1 - core, ref.shape[1])
+        span = ref.shape[0] // pieces
+        for piece in range(pieces):
+            rows = pl.ds(pl.multiple_of(block * BLOCK + base + piece * span, BLOCK // 8), span)
+            copies.append(
+                pltpu.make_async_copy(
+                    ref.at[pl.ds(piece * span, span)],
+                    whole_ref.at[rows, columns],
+                    sem.at[len(copies)],
+                )
+            )
+    return copies
+
+
+def place_count(places):
+    return max(1, sum(PLACE_PARTS if kind == "full" else 1 for kind, *_ in places))
 
 
 def in_parts(count, parts, body):
@@ -236,52 +288,59 @@
     in_parts(BLOCK // TILE, parts, tile)
 
 
-def apply_powers(powers, scale, wide, narrow, parts):
+def apply_powers(powers, scale, wide, narrow):
     def apply(turn, carry):
         last = jnp.where(turn == ITERS - 1, scale, 1.0)
-
-        def tile(place):
-            cols = aligned(place, TILE)
+        for lo in range(0, wide.shape[1], TILE):
+            cols = slice(lo, lo + TILE)
             value = 2.0 * wide[:, cols] - last * dot(
                 powers[ITERS - 1 - turn], narrow[:, cols]
             )
             wide[:, cols] = value
             narrow[:, cols] = value.astype(jnp.bfloat16)
-
-        in_parts(wide.shape[1] // TILE, parts, tile)
         return carry
 
     lax.fori_loop(0, ITERS, apply, 0)
 
 
-def block_damping(damping_ref, step, blocks):
-    return damping_ref[
-        lax.axis_index("hid") * blocks + 2 * step + lax.axis_index("dp") % 2
-    ]
-
-
-def moves(places, refs, whole_ref, sem):
-    core = lax.axis_index("dp") % 2
-    copies = []
-    for turn, (own, back) in enumerate(places):
-        block = 2 * back + (core if own else 1 - core)
-        copies += place_copies(refs[turn], whole_ref, block, sem.at[turn])
-    return copies
-
-
-def block_kernel(parts_at, step, blocks, tokens, spots, places, held, damping_ref, *refs):
+def block_damping(damping_ref, block, blocks):
+    return damping_ref[lax.axis_index("hid") * blocks + block]
+
+
+def own_block(step):
+    return 2 * step + lax.axis_index("dp") % 2
+
+
+def block_kernel(step, blocks, tokens, spots, places, held, damping_ref, *refs):
     parts = len(spots)
     pieces, spread, refs = refs[:parts], refs[parts : parts + 2], refs[parts + 2 :]
     moving, refs = refs[: len(places)], refs[len(places) + held :]
     whole_ref, send_ref, factor, powers, wide, sem = refs
-    copies = moves(places, moving, whole_ref, sem)
+    copies = place_copies(places, moving, whole_ref, sem)
     start_all(copies)
-    damping = block_damping(damping_ref, step, blocks)
+    damping = block_damping(damping_ref, own_block(step), blocks)
     scale = scaled_factor(pieces, None, factor, powers, damping, tokens)
     residual_powers(factor, scale, powers)
     right_side(pieces, spots, spread, None, scale, wide, send_ref, 2)
-    apply_powers(powers, scale, wide, send_ref, parts_at)
+    apply_powers(powers, scale, wide, send_ref)
     wait_all(copies)
+
+
+def solo_kernel(step, blocks, tokens, spots, places, held, damping_ref, *refs):
+    parts = len(spots)
+    pieces, spread, refs = refs[:parts], refs[parts : parts + 2], refs[parts + 2 :]
+    whole_ref, half_ref, *cut_refs = refs[:-4]
+    factor, powers, wide, _ = refs[-4:]
+    block = blocks - 2 + lax.axis_index("dp") // 2 % 2
+    damping = block_damping(damping_ref, block, blocks)
+    scale = scaled_factor(pieces, None, factor, powers, damping, tokens)
+    residual_powers(factor, scale, powers)
+    right_side(pieces, spots, spread, None, scale, wide, half_ref, 2)
+    apply_powers(powers, scale, wide, half_ref)
+    row = 0
+    for cut_ref in cut_refs:
+        cut_ref[...] = half_ref[row : row + cut_ref.shape[0], :]
+        row += cut_ref.shape[0]
 
 
 def early_kernel(step, blocks, tokens, spots, places, held, *refs):
@@ -289,7 +348,7 @@
     pieces, spread, refs = refs[:parts], refs[parts : parts + 2], refs[parts + 2 :]
     moving, refs = refs[: len(places)], refs[len(places) + held :]
     whole_ref, gram_ref, right_ref, sem = refs
-    copies = moves(places, moving, whole_ref, sem)
+    copies = place_copies(places, moving, whole_ref, sem)
     start_all(copies)
     upper_gram(pieces, gram_ref)
     right_side(pieces, spots, spread, None, None, right_ref, None, 2)
@@ -302,13 +361,13 @@
     gram_ref, right_ref, refs = *refs[:2], refs[2:]
     moving, refs = refs[: len(places)], refs[len(places) + held :]
     whole_ref, send_ref, factor, powers, wide, sem = refs
-    copies = moves(places, moving, whole_ref, sem)
+    copies = place_copies(places, moving, whole_ref, sem)
     start_all(copies)
-    damping = block_damping(damping_ref, step, blocks)
+    damping = block_damping(damping_ref, own_block(step), blocks)
     scale = scaled_factor(pieces, gram_ref, factor, powers, damping, tokens)
     residual_powers(factor, scale, powers)
     right_side(pieces, spots, spread, right_ref, scale, wide, send_ref, 2)
-    apply_powers(powers, scale, wide, send_ref, 1)
+    apply_powers(powers, scale, wide, send_ref)
     wait_all(copies)
 
 
@@ -324,7 +383,7 @@
     )(*operands)
 
 
-def block_call(kernel, step, blocks, tokens, damping, pieces, spread, extra, moving, whole):
+def block_call(kernel, name, step, blocks, tokens, damping, pieces, spread, extra, moving, whole):
     width = spread[0].shape[1]
     spots = sorted(pieces)
     held = whole is not None
@@ -335,7 +394,8 @@
     if held:
         operands, specs = operands + [whole], specs + [ANY]
     rows = blocks * BLOCK
-    outs = [jax.ShapeDtypeStruct((rows, width), jnp.bfloat16)]
+    full = width * (2 if name == "solo" else 1)
+    outs = [jax.ShapeDtypeStruct((rows, full), jnp.bfloat16)]
     if damping is None:
         outs.append(jax.ShapeDtypeStruct((BLOCK, BLOCK), jnp.float32))
         outs.append(jax.ShapeDtypeStruct((BLOCK, width), jnp.float32))
@@ -343,27 +403,32 @@
     else:
         outs.append(jax.ShapeDtypeStruct((BLOCK, width), jnp.bfloat16))
         shapes = square_scratch(width)
-    shapes = shapes + [pltpu.SemaphoreType.DMA((2, 4))]
-    kernel = functools.partial(kernel, step, blocks, tokens, spots, list(moving), held)
+    if name == "solo":
+        outs += [jax.ShapeDtypeStruct((rows, width), jnp.bfloat16) for rows in SOLO_CUTS]
+    places = list(moving)
+    shapes = shapes + [pltpu.SemaphoreType.DMA((place_count(places),))]
+    kernel = functools.partial(kernel, step, blocks, tokens, spots, places, held)
     out_specs = [ANY] + [VMEM] * (len(outs) - 1)
     return call(kernel, operands, specs, outs, out_specs, shapes, held)
 
 
-def place_kernel(step, own, source, held_ref, whole_ref, sem):
-    core = lax.axis_index("dp") % 2
-    copies = place_copies(source, whole_ref, 2 * step + (core if own else 1 - core), sem, 8)
+def place_kernel(places, *refs):
+    count = len(places)
+    whole_ref, sem = refs[count + 1 :]
+    copies = place_copies(places, refs[:count], whole_ref, sem)
     start_all(copies)
     wait_all(copies)
 
 
-def place(step, own, source, whole):
+def place(moving, whole):
+    places = list(moving)
     return call(
-        functools.partial(place_kernel, step, own),
-        [source, whole],
-        [VMEM, ANY],
+        functools.partial(place_kernel, places),
+        [*moving.values(), whole],
+        [VMEM] * len(places) + [ANY],
         jax.ShapeDtypeStruct(whole.shape, whole.dtype),
         ANY,
-        [pltpu.SemaphoreType.DMA((8,))],
+        [pltpu.SemaphoreType.DMA((place_count(places),))],
         True,
     )
 
@@ -372,8 +437,9 @@
     span = hidden_acts.shape[0]
     tokens = span * lax.axis_size("dp")
     core = lax.axis_index("dp") % 2
+    chip = lax.axis_index("dp") // 2 % 2
     blocks = hidden_acts.shape[1] // BLOCK
-    steps = blocks // 2
+    steps = step_count(blocks)
     spots = range(1, lax.axis_size("dp"))
 
     small = span // cuts
@@ -383,49 +449,68 @@
     side = swap(out_grads, "dp", 1)
     cross = [swap(over[cut], "dp", 1) for cut in range(cuts)]
 
-    def columns(step, which):
-        return lax.dynamic_slice_in_dim(hidden_acts, (2 * step + which) * BLOCK, BLOCK, 1)
-
+    def columns(block):
+        return lax.dynamic_slice_in_dim(hidden_acts, block * BLOCK, BLOCK, 1)
+
+    if steps * 2 < blocks:
+        mine, theirs = columns(blocks - 2 + chip), columns(blocks - 1 - chip)
+        solo = {0: mine, 1: swap(mine, "dp", 1), 2: swap(theirs, "dp", 2)}
+        solo[3] = swap(solo[2], "dp", 1)
     pieces = []
     for step in range(steps):
-        same, other = columns(step, core), columns(step, 1 - core)
+        same, other = columns(2 * step + core), columns(2 * step + 1 - core)
         pieces.append({0: same})
         for spot in spots:
             pieces[step][spot] = swap(other if spot % 2 else same, "dp", spot)
 
-    spread = precondition_grads([out_grads, side, *over, *cross], cuts, tokens)
-    sends, backs = [], []
+    factor = out_factor_powers([out_grads, side, *over, *cross], cuts, tokens)
+    high, low, high_half, low_half = precondition_grads(*factor)
+    spread = (high, low)
     whole = None
-
-    def moving(step):
-        ready = {}
-        if 1 <= step <= len(sends):
-            ready[True, step - 1] = sends[step - 1]
-        if step >= 2:
-            ready[False, step - 2] = backs[step - 2]
-        return ready
-
+    ready, final = {}, [{} for _ in range(2)]
+    if steps * 2 < blocks:
+        whole, half, *parts = block_call(
+            solo_kernel, "solo", None, blocks, tokens, damping, solo, (high_half, low_half),
+            (), {}, None,
+        )
+        ready["half", True, True, 0] = half
+        upcoming = {("half", True, False, 0): swap(half, "dp", 1)}
+        final += [{}, {}]
+        row = 0
+        for turn, part in enumerate(parts):
+            got = swap(part, "dp", 2)
+            passed = swap(got, "dp", 1)
+            final[2]["half", False, True, row] = got
+            final[turn + 2]["half", False, False, row] = passed
+            row += part.shape[0]
+    else:
+        upcoming = {}
     for step in range(steps - 1):
         whole, send = block_call(
-            functools.partial(block_kernel, 1), step, blocks, tokens, damping, pieces[step], spread, (),
-            moving(step), whole,
+            block_kernel, "block", step, blocks, tokens, damping, pieces[step], spread, (),
+            ready, whole,
         )
-        sends.append(send)
-        backs.append(swap(send, "dp", 1))
+        ready = {("full", True, step): send, **upcoming}
+        upcoming = {("full", False, step): swap(send, "dp", 1)}
     step = steps - 1
     late = {LATE: pieces[step].pop(LATE)}
     whole, gram, right = block_call(
-        early_kernel, step, blocks, tokens, None, pieces[step], spread, (),
-        moving(step), whole,
-    )
-    ready = {(False, step - 1): backs[step - 1]} if step else {}
-    whole, send = block_call(
-        late_kernel, step, blocks, tokens, damping, late, spread, (gram, right),
+        early_kernel, "early", step, blocks, tokens, None, pieces[step], spread, (),
         ready, whole,
     )
-    last = swap(send, "dp", 1)
-    whole = place(step, True, send, whole)
-    return place(step, False, last, whole)
+    whole, send = block_call(
+        late_kernel, "late", step, blocks, tokens, damping, late, spread, (gram, right),
+        upcoming, whole,
+    )
+    final[0]["full", True, step] = send
+    final[1]["full", False, step] = swap(send, "dp", 1)
+    for moving in final:
+        whole = place(moving, whole)
+    return whole
+
+
+def step_count(blocks):
+    return (blocks - 2) // 2 if blocks > 4 else blocks // 2
 
 
 def solution(mesh):

time: 167 us -> 193 us (1.16)
  waiting for transfers between devices: 54.2 us -> 84.1 us
  Pallas kernels: 89.5 us -> 85.4 us
    ppermute x25 -> x29, waiting for transfers between devices: 54.2 us -> 84.1 us  [swap(): return lax.ppermute(value, axis, pairs)]
    pallas_call x7 -> x9, Pallas kernels: 73.4 us -> 69.8 us  [call(): pl.pallas_call(kernel, out_shape=outs, in_specs=specs, out_specs=out_spec...]
    ppermute x25 -> x29, starting transfers between devices: 19.3 us -> 18.7 us  [swap(): return lax.ppermute(value, axis, pairs)]
    pallas_call x1 -> x2, Pallas kernels: 16 us -> 15.6 us  [the longest x1 9.01 us: precondition_grads(): pl.pallas_call(functools.partial(spread_kernel, tokens), out_shape=[jax.S...]
  transfers between devices with their start and end apart: 25 -> 29, of which waited for: 15 -> 13; matrix products, arithmetic and copies ran while one was open for 2% -> 0% of each run, Pallas kernels for 34% -> 37%
where the time goes in v2:
time: 193 us; the launch traced here: 192 us
  Pallas kernels  85.4 us (44%)
  waiting for transfers between devices  84.1 us (44%)
  starting transfers between devices  18.7 us (10%)
  local copies, waits for them, and re-layouts  3.9 us (2%)
    ppermute x29, waiting for transfers between devices, swap(): return lax.ppermute(value, axis, pairs)  84.1 us
    pallas_call x9, Pallas kernels, call(): pl.pallas_call(kernel, out_shape=outs, in_specs=specs, out_specs=out_spec...  69.8 us
    ppermute x29, starting transfers between devices, swap(): return lax.ppermute(value, axis, pairs)  18.7 us
    pallas_call x1, Pallas kernels, precondition_grads(): pl.pallas_call(functools.partial(spread_kernel, tokens), out_shape=[jax.S...  9.01 us
    pallas_call x1, Pallas kernels, out_factor_powers(): pl.pallas_call(functools.partial(out_kernel, cuts, tokens), out_shape=[ja...  6.58 us
    dynamic_slice x1, local copies, waits for them, and re-layouts, columns(): return lax.dynamic_slice_in_dim(hidden_acts, block * BLOCK, BLOCK, 1)  3.87 us
  transfers between devices with their start and end apart: 29, of which 13 were waited for; matrix products, arithmetic and copies ran while one was open for 0% of the time, Pallas kernels for 37%

profile of v2, /device:TPU:0, one launch (start us, length us, event | category | flops | bytes accessed | tf_op | source)
XLA Modules:
  0.0 192.4 jit_solution(7271795008922610697)
XLA Ops:
  0.0 3.9 %constant_dynamic-slice_fusion = (bf16[256,1024]{1,0:T(8,128)(2,1)}, bf16[256,1024]{1,0:T(8,128)(2,1)}, bf16[256,1024]{1,0:T(8,128)(2,1)S(1)}, bf16[256,1024]{1,...) fusion(bf16[256,8192]{1,0:T(8,128)(2,1)} %param.3, ...), kind=kLoop, calls=%fused_computation | loop fusion | bytes 8388640 | tf_op jit(solution)/shard_map/dynamic_slice | solution.py:453
  3.9 3.0 %collective-permute-start.1 = (bf16[256,1024]{1,0:T(8,128)(2,1)}, bf16[256,1024]{1,0:T(8,128)(2,1)S(1)}, u32[]{:S(2)}, u32[]{:S(2)}) collective-permute-start(bf16[256,1024]{1,0:T(8,128)(2,1)} %get-tuple-element.50), channel_id=1, source_target_pairs={{0,2},{1,3},{2,0},{3,1},{4,6},{5,7},{6,4},{7,5},{8,10},{9,11},{10,... | collective-permute-start | bytes 1572872 | tf_op jit(solution)/shard_map/ppermute | solution.py:35
  6.9 14.8 %collective-permute-done.4.refs_2_ = bf16[64,1024]{1,0:T(8,128)(2,1)S(1)} collective-permute-done((bf16[64,1024]{1,0:T(8,128)(2,1)S(1)}, bf16[64,1024]{1,0:T(8,128)(2,1)S(1)}, u32[]{:S(2)}, u32[]{:S(2)}) %collective-permute-start.4) | collective-permute-done | bytes 131104 | tf_op jit(solution)/shard_map/ppermute | solution.py:35
  21.8 1.8 collective-permute-start.6
  26.7 1.9 %collective-permute-start.5 = (bf16[64,1024]{1,0:T(8,128)(2,1)S(1)}, bf16[64,1024]{1,0:T(8,128)(2,1)S(1)}, u32[]{:S(2)}, u32[]{:S(2)}) collective-permute-start(bf16[64,1024]{1,0:T(8,128)(2,1)S(1)} %collective-permute-done.4.refs_2_), channel_id=1, source_target_pairs={{0,4},{4,0},{8,12},{12,8},{16,20},{20,16},{24,28},{28,24},{1,5},{5... | collective-permute-start | bytes 393224 | tf_op jit(solution)/shard_map/ppermute | solution.py:35
  28.7 2.4 %collective-permute-done.7.refs_5_ = bf16[64,1024]{1,0:T(8,128)(2,1)S(1)} collective-permute-done((bf16[64,1024]{1,0:T(8,128)(2,1)S(1)}, bf16[64,1024]{1,0:T(8,128)(2,1)S(1)}, u32[]{:S(2)}, u32[]{:S(2)}) %collective-permute-start.7) | collective-permute-done | bytes 131104 | tf_op jit(solution)/shard_map/ppermute | solution.py:35
  31.0 2.7 %collective-permute-done.5.refs_3_ = bf16[64,1024]{1,0:T(8,128)(2,1)S(1)} collective-permute-done((bf16[64,1024]{1,0:T(8,128)(2,1)S(1)}, bf16[64,1024]{1,0:T(8,128)(2,1)S(1)}, u32[]{:S(2)}, u32[]{:S(2)}) %collective-permute-start.5) | collective-permute-done | bytes 131104 | tf_op jit(solution)/shard_map/ppermute | solution.py:35
  36.4 1.5 collective-permute-start.23
  37.9 6.6 %out_factor.1 = (bf16[1024,1024]{1,0:T(8,128)(2,1)S(1)}, bf16[3,1024,1024]{2,1,0:T(8,128)(2,1)S(1)}, f32[8,128]{1,0:T(8,128)S(1)}) custom-call(bf16[256,1024]{1,0:T(8,128)(2,1)S(1)} %copy-done, bf16[256,1024]{1,0:T(8,128)(2,1)S(1)} %collective-permute-done.3.refs_1_, bf16[64,1024]{1,0:T(8,128)(2,1)S(1)} %collective-permute-done.4.refs_2_, ...), custom_call_target="tpu_custom_call" | custom-call | tf_op jit(solution)/shard_map/out_factor/pallas_call | solution.py:185
  44.5 9.0 %out_spread.1 = (bf16[1024,1024]{1,0:T(8,128)(2,1)S(1)}, bf16[1024,1024]{1,0:T(8,128)(2,1)S(1)}, bf16[1024,512]{1,0:T(8,128)(2,1)S(1)}, bf16[1024,512]{1,0:T(8,128)(2,1)S(1)}) custom-call(bf16[1024,1024]{1,0:T(8,128)(2,1)S(1)} %get-tuple-element.25.given, bf16[3,1024,1024]{2,1,0:T(8,128)(2,1)S(1)} %get-tuple-element.26.powers, ...), custom_call_target="tpu_custom_call" | custom-call | tf_op jit(solution)/shard_map/out_spread/pallas_call | solution.py:205
  53.6 12.1 %shard_map.37 = (bf16[8192,1024]{1,0:T(8,128)(2,1)}, bf16[1024,512]{1,0:T(8,128)(2,1)S(1)}, bf16[768,512]{1,0:T(8,128)(2,1)S(1)}, bf16[256,512]{1,0:T(8,128)(2,1)S(1)}) custom-call(f32[64]{0:T(128)S(1)} %copy-done.1, bf16[256,1024]{1,0:T(8,128)(2,1)S(1)} %get-tuple-element.51.refs_0_, bf16[256,1024]{1,0:T(8,128)(2,1)S(1)} %collective-permute-done.refs_1_, ...), custom_call_target="tpu_custom_call" | custom-call | tf_op jit(solution)/shard_map/pallas_call | solution.py:375
  66.5 1.5 collective-permute-start.20
  68.3 11.2 %collective-permute-done.24.refs_3_ = bf16[256,1024]{1,0:T(8,128)(2,1)S(1)} collective-permute-done((bf16[256,1024]{1,0:T(8,128)(2,1)S(1)}, bf16[256,1024]{1,0:T(8,128)(2,1)S(1)}, u32[]{:S(2)}, u32[]{:S(2)}) %collective-permute-start.24) | collective-permute-done | bytes 524320 | tf_op jit(solution)/shard_map/ppermute | solution.py:35
  79.5 17.3 %shard_map.38 = (bf16[8192,1024]{1,0:T(8,128)(2,1)}, bf16[1024,1024]{1,0:T(8,128)(2,1)S(1)}) custom-call(f32[64]{0:T(128)S(1)} %copy-done.1, bf16[256,1024]{1,0:T(8,128)(2,1)S(1)} %get-tuple-element.52.refs_0_, bf16[256,1024]{1,0:T(8,128)(2,1)S(1)} %collective-permute-done.22.refs_1_, ...), custom_call_target="tpu_custom_call", output_to_operand_aliasing={{0}: (8, {})} | custom-call | tf_op jit(solution)/shard_map/pallas_call | solution.py:375
  97.8 4.1 %collective-permute-done.21.refs_3_ = bf16[256,1024]{1,0:T(8,128)(2,1)S(1)} collective-permute-done((bf16[256,1024]{1,0:T(8,128)(2,1)S(1)}, bf16[256,1024]{1,0:T(8,128)(2,1)S(1)}, u32[]{:S(2)}, u32[]{:S(2)}) %collective-permute-start.21) | collective-permute-done | bytes 524320 | tf_op jit(solution)/shard_map/ppermute | solution.py:35
  101.9 17.5 %shard_map.39 = (bf16[8192,1024]{1,0:T(8,128)(2,1)}, bf16[1024,1024]{1,0:T(8,128)(2,1)S(1)}) custom-call(f32[64]{0:T(128)S(1)} %copy-done.1, bf16[256,1024]{1,0:T(8,128)(2,1)S(1)} %get-tuple-element.47.refs_0_, bf16[256,1024]{1,0:T(8,128)(2,1)S(1)} %collective-permute-done.19.refs_1_, ...), custom_call_target="tpu_custom_call", output_to_operand_aliasing={{0}: (9, {})} | custom-call | tf_op jit(solution)/shard_map/pallas_call | solution.py:375
  120.6 1.5 collective-permute-start.16
  122.1 2.4 %collective-permute-done.17.refs_1_ = bf16[256,1024]{1,0:T(8,128)(2,1)S(1)} collective-permute-done((bf16[256,1024]{1,0:T(8,128)(2,1)S(1)}, bf16[256,1024]{1,0:T(8,128)(2,1)S(1)}, u32[]{:S(2)}, u32[]{:S(2)}) %collective-permute-start.17) | collective-permute-done | bytes 524320 | tf_op jit(solution)/shard_map/ppermute | solution.py:35
  124.5 9.2 %collective-permute-done.18.refs_2_ = bf16[256,1024]{1,0:T(8,128)(2,1)S(1)} collective-permute-done((bf16[256,1024]{1,0:T(8,128)(2,1)S(1)}, bf16[256,1024]{1,0:T(8,128)(2,1)S(1)}, u32[]{:S(2)}, u32[]{:S(2)}) %collective-permute-start.18) | collective-permute-done | bytes 524320 | tf_op jit(solution)/shard_map/ppermute | solution.py:35
  133.7 5.0 %shard_map.40 = (bf16[8192,1024]{1,0:T(8,128)(2,1)}, f32[1024,1024]{1,0:T(8,128)S(1)}, f32[1024,1024]{1,0:T(8,128)S(1)}) custom-call(bf16[256,1024]{1,0:T(8,128)(2,1)S(1)} %get-tuple-element.49.refs_0_, bf16[256,1024]{1,0:T(8,128)(2,1)S(1)} %collective-permute-done.17.refs_1_, ...), custom_call_target="tpu_custom_call", output_to_operand_aliasing={{0}: (7, {})} | custom-call | tf_op jit(solution)/shard_map/pallas_call | solution.py:375
  138.7 6.8 %collective-permute-done.16.refs_0_ = bf16[256,1024]{1,0:T(8,128)(2,1)S(1)} collective-permute-done((bf16[256,1024]{1,0:T(8,128)(2,1)S(1)}, bf16[256,1024]{1,0:T(8,128)(2,1)S(1)}, u32[]{:S(2)}, u32[]{:S(2)}) %collective-permute-start.16) | collective-permute-done | bytes 524320 | tf_op jit(solution)/shard_map/ppermute | solution.py:35
  145.5 13.2 %shard_map.41 = (bf16[8192,1024]{1,0:T(8,128)(2,1)}, bf16[1024,1024]{1,0:T(8,128)(2,1)S(1)}) custom-call(f32[64]{0:T(128)S(1)} %copy-done.1, bf16[256,1024]{1,0:T(8,128)(2,1)S(1)} %collective-permute-done.16.refs_0_, bf16[1024,1024]{1,0:T(8,128)(2,1)S(1)} %get-tuple-element.32.refs_4_.refs_3_.refs_1_, ...), custom_call_target="tpu_custom_call", output_to_operand_aliasing={{0}: (7, {})} | custom-call | tf_op jit(solution)/shard_map/pallas_call | solution.py:375
  159.4 19.3 %collective-permute-done.14.refs_0_ = bf16[768,512]{1,0:T(8,128)(2,1)S(1)} collective-permute-done((bf16[768,512]{1,0:T(8,128)(2,1)S(1)}, bf16[768,512]{1,0:T(8,128)(2,1)S(1)}, u32[]{:S(2)}, u32[]{:S(2)}) %collective-permute-start.14) | collective-permute-done | bytes 786464 | tf_op jit(solution)/shard_map/ppermute | solution.py:35
  179.3 8.2 %collective-permute-done.12.refs_2_ = bf16[256,512]{1,0:T(8,128)(2,1)S(1)} collective-permute-done((bf16[256,512]{1,0:T(8,128)(2,1)S(1)}, bf16[256,512]{1,0:T(8,128)(2,1)S(1)}, u32[]{:S(2)}, u32[]{:S(2)}) %collective-permute-start.12) | collective-permute-done | bytes 262176 | tf_op jit(solution)/shard_map/ppermute | solution.py:35
  (57 shorter events, 15.2 us)
Async XLA Ops:
  3.9 20.2 %collective-permute-start.1 = (bf16[256,1024]{1,0:T(8,128)(2,1)}, bf16[256,1024]{1,0:T(8,128)(2,1)S(1)}, u32[]{:S(2)}, u32[]{:S(2)}) collective-permute-start(bf16[256,1024]{1,0:T(8,128)(2,1)} %get-tuple-element.50), channel_id=1, source_target_pairs={{0,2},{1,3},{2,0},{3,1},{4,6},{5,7},{6,4},{7,5},{8,10},{9,11},{10,... | collective-permute-start | bytes 1572872 | tf_op jit(solution)/shard_map/ppermute | solution.py:35
  6.9 14.9 %collective-permute-start.4 = (bf16[64,1024]{1,0:T(8,128)(2,1)S(1)}, bf16[64,1024]{1,0:T(8,128)(2,1)S(1)}, u32[]{:S(2)}, u32[]{:S(2)}) collective-permute-start(bf16[64,1024]{1,0:T(8,128)(2,1)S(1)} %constant_dynamic-slice_fusion.6), channel_id=1, source_target_pairs={{0,2},{1,3},{2,0},{3,1},{4,6},{5,7},{6,4},{7,5},{8,10},{9,11},{10,... | collective-permute-start | bytes 393224 | tf_op jit(solution)/shard_map/ppermute | solution.py:35
  21.8 5.0 %collective-permute-start.6 = (bf16[64,1024]{1,0:T(8,128)(2,1)S(1)}, bf16[64,1024]{1,0:T(8,128)(2,1)S(1)}, u32[]{:S(2)}, u32[]{:S(2)}) collective-permute-start(bf16[64,1024]{1,0:T(8,128)(2,1)S(1)} %collective-permute-done.4.refs_2_), channel_id=1, source_target_pairs={{0,8},{4,12},{8,0},{12,4},{16,24},{20,28},{24,16},{28,20},{1,9},{5... | collective-permute-start | bytes 393224 | tf_op jit(solution)/shard_map/ppermute | solution.py:35
  23.6 14.3 %collective-permute-start.3 = (bf16[256,1024]{1,0:T(8,128)(2,1)S(1)}, bf16[256,1024]{1,0:T(8,128)(2,1)S(1)}, u32[]{:S(2)}, u32[]{:S(2)}) collective-permute-start(bf16[256,1024]{1,0:T(8,128)(2,1)S(1)} %copy-done), channel_id=1, source_target_pairs={{0,1},{1,0},{2,3},{3,2},{4,5},{5,4},{6,7},{7,6},{8,9},{9,8},{10,11... | collective-permute-start | bytes 1572872 | tf_op jit(solution)/shard_map/ppermute | solution.py:35
  23.6 30.0 %collective-permute-start = (bf16[256,1024]{1,0:T(8,128)(2,1)S(1)}, bf16[256,1024]{1,0:T(8,128)(2,1)S(1)}, u32[]{:S(2)}, u32[]{:S(2)}) collective-permute-start(bf16[256,1024]{1,0:T(8,128)(2,1)S(1)} %get-tuple-element.51.refs_0_), channel_id=1, source_target_pairs={{0,1},{1,0},{2,3},{3,2},{4,5},{5,4},{6,7},{7,6},{8,9},{9,8},{10,11... | collective-permute-start | bytes 1572872 | tf_op jit(solution)/shard_map/ppermute | solution.py:35
  24.1 29.5 %collective-permute-start.2 = (bf16[256,1024]{1,0:T(8,128)(2,1)S(1)}, bf16[256,1024]{1,0:T(8,128)(2,1)S(1)}, u32[]{:S(2)}, u32[]{:S(2)}) collective-permute-start(bf16[256,1024]{1,0:T(8,128)(2,1)S(1)} %collective-permute-done.1.refs_2_), channel_id=1, source_target_pairs={{0,1},{1,0},{2,3},{3,2},{4,5},{5,4},{6,7},{7,6},{8,9},{9,8},{10,11... | collective-permute-start | bytes 1572872 | tf_op jit(solution)/shard_map/ppermute | solution.py:35
  24.1 6.9 %collective-permute-start.7 = (bf16[64,1024]{1,0:T(8,128)(2,1)S(1)}, bf16[64,1024]{1,0:T(8,128)(2,1)S(1)}, u32[]{:S(2)}, u32[]{:S(2)}) collective-permute-start(bf16[64,1024]{1,0:T(8,128)(2,1)S(1)} %collective-permute-done.4.refs_2_), channel_id=1, source_target_pairs={{0,12},{4,8},{8,4},{12,0},{16,28},{20,24},{24,20},{28,16},{1,13},{... | collective-permute-start | bytes 393224 | tf_op jit(solution)/shard_map/ppermute | solution.py:35
  26.7 7.0 %collective-permute-start.5 = (bf16[64,1024]{1,0:T(8,128)(2,1)S(1)}, bf16[64,1024]{1,0:T(8,128)(2,1)S(1)}, u32[]{:S(2)}, u32[]{:S(2)}) collective-permute-start(bf16[64,1024]{1,0:T(8,128)(2,1)S(1)} %collective-permute-done.4.refs_2_), channel_id=1, source_target_pairs={{0,4},{4,0},{8,12},{12,8},{16,20},{20,16},{24,28},{28,24},{1,5},{5... | collective-permute-start | bytes 393224 | tf_op jit(solution)/shard_map/ppermute | solution.py:35
  35.3 31.2 %collective-permute-start.22 = (bf16[256,1024]{1,0:T(8,128)(2,1)}, bf16[256,1024]{1,0:T(8,128)(2,1)S(1)}, u32[]{:S(2)}, u32[]{:S(2)}) collective-permute-start(bf16[256,1024]{1,0:T(8,128)(2,1)} %get-tuple-element.45), channel_id=1, source_target_pairs={{0,1},{1,0},{2,3},{3,2},{4,5},{5,4},{6,7},{7,6},{8,9},{9,8},{10,11... | collective-permute-start | bytes 1572872 | tf_op jit(solution)/shard_map/ppermute | solution.py:35
  36.4 31.6 %collective-permute-start.23 = (bf16[256,1024]{1,0:T(8,128)(2,1)S(1)}, bf16[256,1024]{1,0:T(8,128)(2,1)S(1)}, u32[]{:S(2)}, u32[]{:S(2)}) collective-permute-start(bf16[256,1024]{1,0:T(8,128)(2,1)S(1)} %get-tuple-element.52.refs_0_), channel_id=1, source_target_pairs={{0,2},{1,3},{2,0},{3,1},{4,6},{5,7},{6,4},{7,5},{8,10},{9,11},{10,... | collective-permute-start | bytes 1572872 | tf_op jit(solution)/shard_map/ppermute | solution.py:35
  65.7 36.2 %collective-permute-start.25 = (bf16[1024,512]{1,0:T(8,128)(2,1)S(1)}, bf16[1024,512]{1,0:T(8,128)(2,1)S(1)}, u32[]{:S(2)}, u32[]{:S(2)}) collective-permute-start(bf16[1024,512]{1,0:T(8,128)(2,1)S(1)} %get-tuple-element.34.refs_6_), channel_id=1, source_target_pairs={{0,1},{1,0},{2,3},{3,2},{4,5},{5,4},{6,7},{7,6},{8,9},{9,8},{10,11... | collective-permute-start | bytes 3145736 | tf_op jit(solution)/shard_map/ppermute | solution.py:35
  65.8 13.7 %collective-permute-start.24 = (bf16[256,1024]{1,0:T(8,128)(2,1)S(1)}, bf16[256,1024]{1,0:T(8,128)(2,1)S(1)}, u32[]{:S(2)}, u32[]{:S(2)}) collective-permute-start(bf16[256,1024]{1,0:T(8,128)(2,1)S(1)} %copy-done.4), channel_id=1, source_target_pairs={{0,3},{1,2},{2,1},{3,0},{4,7},{5,6},{6,5},{7,4},{8,11},{9,10},{10,... | collective-permute-start | bytes 1572872 | tf_op jit(solution)/shard_map/ppermute | solution.py:35
  66.4 31.4 %collective-permute-start.19 = (bf16[256,1024]{1,0:T(8,128)(2,1)S(1)}, bf16[256,1024]{1,0:T(8,128)(2,1)S(1)}, u32[]{:S(2)}, u32[]{:S(2)}) collective-permute-start(bf16[256,1024]{1,0:T(8,128)(2,1)S(1)} %copy-done.3), channel_id=1, source_target_pairs={{0,1},{1,0},{2,3},{3,2},{4,5},{5,4},{6,7},{7,6},{8,9},{9,8},{10,11... | collective-permute-start | bytes 1572872 | tf_op jit(solution)/shard_map/ppermute | solution.py:35
  66.5 31.3 %collective-permute-start.20 = (bf16[256,1024]{1,0:T(8,128)(2,1)S(1)}, bf16[256,1024]{1,0:T(8,128)(2,1)S(1)}, u32[]{:S(2)}, u32[]{:S(2)}) collective-permute-start(bf16[256,1024]{1,0:T(8,128)(2,1)S(1)} %get-tuple-element.47.refs_0_), channel_id=1, source_target_pairs={{0,2},{1,3},{2,0},{3,1},{4,6},{5,7},{6,4},{7,5},{8,10},{9,11},{10,... | collective-permute-start | bytes 1572872 | tf_op jit(solution)/shard_map/ppermute | solution.py:35
  68.0 33.9 %collective-permute-start.21 = (bf16[256,1024]{1,0:T(8,128)(2,1)S(1)}, bf16[256,1024]{1,0:T(8,128)(2,1)S(1)}, u32[]{:S(2)}, u32[]{:S(2)}) collective-permute-start(bf16[256,1024]{1,0:T(8,128)(2,1)S(1)} %copy-done.3), channel_id=1, source_target_pairs={{0,3},{1,2},{2,1},{3,0},{4,7},{5,6},{6,5},{7,4},{8,11},{9,10},{10,... | collective-permute-start | bytes 1572872 | tf_op jit(solution)/shard_map/ppermute | solution.py:35
  96.7 37.0 %collective-permute-start.26 = (bf16[1024,1024]{1,0:T(8,128)(2,1)S(1)}, bf16[1024,1024]{1,0:T(8,128)(2,1)S(1)}, u32[]{:S(2)}, u32[]{:S(2)}) collective-permute-start(bf16[1024,1024]{1,0:T(8,128)(2,1)S(1)} %get-tuple-element.36.refs_6_), channel_id=1, source_target_pairs={{0,1},{1,0},{2,3},{3,2},{4,5},{5,4},{6,7},{7,6},{8,9},{9,8},{10,11... | collective-permute-start | bytes 6291464 | tf_op jit(solution)/shard_map/ppermute | solution.py:35
  119.5 26.0 %collective-permute-start.27 = (bf16[1024,1024]{1,0:T(8,128)(2,1)S(1)}, bf16[1024,1024]{1,0:T(8,128)(2,1)S(1)}, u32[]{:S(2)}, u32[]{:S(2)}) collective-permute-start(bf16[1024,1024]{1,0:T(8,128)(2,1)S(1)} %get-tuple-element.38.refs_5_), channel_id=1, source_target_pairs={{0,1},{1,0},{2,3},{3,2},{4,5},{5,4},{6,7},{7,6},{8,9},{9,8},{10,11... | collective-permute-start | bytes 6291464 | tf_op jit(solution)/shard_map/ppermute | solution.py:35
  120.0 4.5 %collective-permute-start.17 = (bf16[256,1024]{1,0:T(8,128)(2,1)S(1)}, bf16[256,1024]{1,0:T(8,128)(2,1)S(1)}, u32[]{:S(2)}, u32[]{:S(2)}) collective-permute-start(bf16[256,1024]{1,0:T(8,128)(2,1)S(1)} %copy-done.2), channel_id=1, source_target_pairs={{0,1},{1,0},{2,3},{3,2},{4,5},{5,4},{6,7},{7,6},{8,9},{9,8},{10,11... | collective-permute-start | bytes 1572872 | tf_op jit(solution)/shard_map/ppermute | solution.py:35
  120.0 13.6 %collective-permute-start.18 = (bf16[256,1024]{1,0:T(8,128)(2,1)S(1)}, bf16[256,1024]{1,0:T(8,128)(2,1)S(1)}, u32[]{:S(2)}, u32[]{:S(2)}) collective-permute-start(bf16[256,1024]{1,0:T(8,128)(2,1)S(1)} %copy-done.2), channel_id=1, source_target_pairs={{0,3},{1,2},{2,1},{3,0},{4,7},{5,6},{6,5},{7,4},{8,11},{9,10},{10,... | collective-permute-start | bytes 1572872 | tf_op jit(solution)/shard_map/ppermute | solution.py:35
  120.6 24.9 %collective-permute-start.16 = (bf16[256,1024]{1,0:T(8,128)(2,1)S(1)}, bf16[256,1024]{1,0:T(8,128)(2,1)S(1)}, u32[]{:S(2)}, u32[]{:S(2)}) collective-permute-start(bf16[256,1024]{1,0:T(8,128)(2,1)S(1)} %get-tuple-element.49.refs_0_), channel_id=1, source_target_pairs={{0,2},{1,3},{2,0},{3,1},{4,6},{5,7},{6,4},{7,5},{8,10},{9,11},{10,... | collective-permute-start | bytes 1572872 | tf_op jit(solution)/shard_map/ppermute | solution.py:35
  158.7 30.1 %collective-permute-start.28 = (bf16[1024,1024]{1,0:T(8,128)(2,1)S(1)}, bf16[1024,1024]{1,0:T(8,128)(2,1)S(1)}, u32[]{:S(2)}, u32[]{:S(2)}) collective-permute-start(bf16[1024,1024]{1,0:T(8,128)(2,1)S(1)} %get-tuple-element.43.refs_0_), channel_id=1, source_target_pairs={{0,1},{1,0},{2,3},{3,2},{4,5},{5,4},{6,7},{7,6},{8,9},{9,8},{10,11... | collective-permute-start | bytes 6291464 | tf_op jit(solution)/shard_map/ppermute | solution.py:35
  158.8 19.9 %collective-permute-start.14 = (bf16[768,512]{1,0:T(8,128)(2,1)S(1)}, bf16[768,512]{1,0:T(8,128)(2,1)S(1)}, u32[]{:S(2)}, u32[]{:S(2)}) collective-permute-start(bf16[768,512]{1,0:T(8,128)(2,1)S(1)} %get-tuple-element.31), channel_id=1, source_target_pairs={{0,2},{1,3},{2,0},{3,1},{4,6},{5,7},{6,4},{7,5},{8,10},{9,11},{10,... | collective-permute-start | bytes 2359304 | tf_op jit(solution)/shard_map/ppermute | solution.py:35
  178.7 11.5 %collective-permute-start.15 = (bf16[768,512]{1,0:T(8,128)(2,1)S(1)}, bf16[768,512]{1,0:T(8,128)(2,1)S(1)}, u32[]{:S(2)}, u32[]{:S(2)}) collective-permute-start(bf16[768,512]{1,0:T(8,128)(2,1)S(1)} %collective-permute-done.14.refs_0_), channel_id=1, source_target_pairs={{0,1},{1,0},{2,3},{3,2},{4,5},{5,4},{6,7},{7,6},{8,9},{9,8},{10,11... | collective-permute-start | bytes 2359304 | tf_op jit(solution)/shard_map/ppermute | solution.py:35
  178.8 8.7 %collective-permute-start.12 = (bf16[256,512]{1,0:T(8,128)(2,1)S(1)}, bf16[256,512]{1,0:T(8,128)(2,1)S(1)}, u32[]{:S(2)}, u32[]{:S(2)}) collective-permute-start(bf16[256,512]{1,0:T(8,128)(2,1)S(1)} %get-tuple-element.30), channel_id=1, source_target_pairs={{0,2},{1,3},{2,0},{3,1},{4,6},{5,7},{6,4},{7,5},{8,10},{9,11},{10,... | collective-permute-start | bytes 786440 | tf_op jit(solution)/shard_map/ppermute | solution.py:35
  (10 other events, 70.0 us)

commit v3 on v2

--- a/solution.py
+++ b/solution.py
@@ -99,11 +99,12 @@
     lax.fori_loop(0, ITERS - 1, square, 0)
 
 
-def out_kernel(cuts, tokens, *refs):
+def out_kernel(cuts, tokens, begun, *refs):
     span = tokens // 4
     count = 2 + 2 * cuts
     pieces = refs[:count]
-    grads, powers, scale_ref, factor, sem = refs[count:]
+    prior = refs[count] if begun else None
+    grads, powers, scale_ref, factor, sem = refs[count + begun :]
     hid = lax.axis_index("hid")
     small = span // cuts
     starts = [0, span]
@@ -120,7 +121,8 @@
     ]
     start_all(copies)
     wait_all(copies)
-    scale = scaled_factor([grads], None, factor, powers, OUT_DAMPING, tokens)
+    left = [grads.at[2 * span :]] if begun else [grads]
+    scale = scaled_factor(left, prior, factor, powers, OUT_DAMPING, tokens)
     scale_ref[...] = jnp.broadcast_to(scale, scale_ref.shape)
     residual_powers(factor, scale, powers)
 
@@ -180,16 +182,17 @@
         copy.wait()
 
 
-def out_factor_powers(pieces, cuts, tokens):
+def out_factor_powers(pieces, prior, cuts, tokens):
     width = pieces[0].shape[1]
+    operands = [*pieces, *prior]
     return pl.pallas_call(
-        functools.partial(out_kernel, cuts, tokens),
+        functools.partial(out_kernel, cuts, tokens, len(prior)),
         out_shape=[
             jax.ShapeDtypeStruct((tokens, width), jnp.bfloat16),
             jax.ShapeDtypeStruct((ITERS, width, width), jnp.bfloat16),
             jax.ShapeDtypeStruct((8, 128), jnp.float32),
         ],
-        in_specs=[VMEM] * len(pieces),
+        in_specs=[VMEM] * len(operands),
         out_specs=[VMEM] * 3,
         scratch_shapes=[
             pltpu.VMEM((width, width), jnp.float32),
@@ -197,7 +200,26 @@
         ],
         compiler_params=pltpu.CompilerParams(vmem_limit_bytes=KERNEL_VMEM),
         name="out_factor",
-    )(*pieces)
+    )(*operands)
+
+
+def begin_kernel(*refs):
+    count = len(refs) // 3
+    for place in range(count):
+        upper_gram(refs[2 * place : 2 * place + 2], refs[2 * count + place])
+
+
+def begin_grams(pairs):
+    operands = [piece for pair in pairs for piece in pair]
+    width = operands[0].shape[1]
+    return pl.pallas_call(
+        begin_kernel,
+        out_shape=[jax.ShapeDtypeStruct((width, width), jnp.float32)] * len(pairs),
+        in_specs=[VMEM] * len(operands),
+        out_specs=[VMEM] * len(pairs),
+        compiler_params=pltpu.CompilerParams(vmem_limit_bytes=KERNEL_VMEM),
+        name="begin",
+    )(*operands)
 
 
 def precondition_grads(grads, powers, scale):
@@ -311,29 +333,31 @@
     return 2 * step + lax.axis_index("dp") % 2
 
 
-def block_kernel(step, blocks, tokens, spots, places, held, damping_ref, *refs):
+def block_kernel(begun, step, blocks, tokens, spots, places, held, damping_ref, *refs):
     parts = len(spots)
     pieces, spread, refs = refs[:parts], refs[parts : parts + 2], refs[parts + 2 :]
+    prior, refs = (refs[0] if begun else None), refs[begun:]
     moving, refs = refs[: len(places)], refs[len(places) + held :]
     whole_ref, send_ref, factor, powers, wide, sem = refs
     copies = place_copies(places, moving, whole_ref, sem)
     start_all(copies)
     damping = block_damping(damping_ref, own_block(step), blocks)
-    scale = scaled_factor(pieces, None, factor, powers, damping, tokens)
+    scale = scaled_factor(pieces[2 * begun :], prior, factor, powers, damping, tokens)
     residual_powers(factor, scale, powers)
     right_side(pieces, spots, spread, None, scale, wide, send_ref, 2)
     apply_powers(powers, scale, wide, send_ref)
     wait_all(copies)
 
 
-def solo_kernel(step, blocks, tokens, spots, places, held, damping_ref, *refs):
+def solo_kernel(begun, step, blocks, tokens, spots, places, held, damping_ref, *refs):
     parts = len(spots)
     pieces, spread, refs = refs[:parts], refs[parts : parts + 2], refs[parts + 2 :]
+    prior, refs = (refs[0] if begun else None), refs[begun:]
     whole_ref, half_ref, *cut_refs = refs[:-4]
     factor, powers, wide, _ = refs[-4:]
     block = blocks - 2 + lax.axis_index("dp") // 2 % 2
     damping = block_damping(damping_ref, block, blocks)
-    scale = scaled_factor(pieces, None, factor, powers, damping, tokens)
+    scale = scaled_factor(pieces[2 * begun :], prior, factor, powers, damping, tokens)
     residual_powers(factor, scale, powers)
     right_side(pieces, spots, spread, None, scale, wide, half_ref, 2)
     apply_powers(powers, scale, wide, half_ref)
@@ -463,15 +487,18 @@
         for spot in spots:
             pieces[step][spot] = swap(other if spot % 2 else same, "dp", spot)
 
-    factor = out_factor_powers([out_grads, side, *over, *cross], cuts, tokens)
+    begun = []
+    if steps * 2 < blocks:
+        begun = begin_grams([(out_grads, side), (solo[0], solo[1]), (pieces[0][0], pieces[0][1])])
+    factor = out_factor_powers([out_grads, side, *over, *cross], begun[:1], cuts, tokens)
     high, low, high_half, low_half = precondition_grads(*factor)
     spread = (high, low)
     whole = None
     ready, final = {}, [{} for _ in range(2)]
     if steps * 2 < blocks:
         whole, half, *parts = block_call(
-            solo_kernel, "solo", None, blocks, tokens, damping, solo, (high_half, low_half),
-            (), {}, None,
+            functools.partial(solo_kernel, 1), "solo", None, blocks, tokens, damping, solo,
+            (high_half, low_half), begun[1:2], {}, None,
         )
         ready["half", True, True, 0] = half
         upcoming = {("half", True, False, 0): swap(half, "dp", 1)}
@@ -480,16 +507,17 @@
         for turn, part in enumerate(parts):
             got = swap(part, "dp", 2)
             passed = swap(got, "dp", 1)
-            final[2]["half", False, True, row] = got
+            final[2 * turn]["half", False, True, row] = got
             final[turn + 2]["half", False, False, row] = passed
             row += part.shape[0]
     else:
         upcoming = {}
     for step in range(steps - 1):
         whole, send = block_call(
-            block_kernel, "block", step, blocks, tokens, damping, pieces[step], spread, (),
-            ready, whole,
+            functools.partial(block_kernel, len(begun[2:])), "block", step, blocks, tokens,
+            damping, pieces[step], spread, begun[2:], ready, whole,
         )
+        begun = []
         ready = {("full", True, step): send, **upcoming}
         upcoming = {("full", False, step): swap(send, "dp", 1)}
     step = steps - 1

time: 193 us -> 196 us (1.016)
    pallas_call x1 -> x2, Pallas kernels: 6.58 us -> 8.45 us  [the longest x1 6.18 us: out_factor_powers(): pl.pallas_call(functools.partial(out_kernel, cuts, tokens, len(prior)), o...]
  transfers between devices with their start and end apart: 29 -> 29, of which waited for: 13 -> 11; matrix products, arithmetic and copies ran while one was open for 0% -> 0% of each run, Pallas kernels for 37% -> 37%
where the time goes in v3:
time: 196 us
  Pallas kernels  86.1 us (44%)
  waiting for transfers between devices  85.6 us (44%)
  starting transfers between devices  19.9 us (10%)
  local copies, waits for them, and re-layouts  3.9 us (2%)
    ppermute x29, waiting for transfers between devices, swap(): return lax.ppermute(value, axis, pairs)  85.6 us
    pallas_call x9, Pallas kernels, call(): pl.pallas_call(kernel, out_shape=outs, in_specs=specs, out_specs=out_spec...  68.7 us
    ppermute x29, starting transfers between devices, swap(): return lax.ppermute(value, axis, pairs)  19.9 us
    pallas_call x1, Pallas kernels, precondition_grads(): pl.pallas_call(functools.partial(spread_kernel, tokens), out_shape=[jax.S...  8.98 us
    pallas_call x1, Pallas kernels, out_factor_powers(): pl.pallas_call(functools.partial(out_kernel, cuts, tokens, len(prior)), o...  6.18 us
  transfers between devices with their start and end apart: 29, of which 11 were waited for; matrix products, arithmetic and copies ran while one was open for 0% of the time, Pallas kernels for 37%

profile of v3, /device:TPU:0, one launch (start us, length us, event | category | flops | bytes accessed | tf_op | source)
XLA Modules:
  0.0 195.9 jit_solution(3177831720885893934)
XLA Ops:
  0.0 3.9 %constant_dynamic-slice_fusion = (bf16[256,1024]{1,0:T(8,128)(2,1)}, bf16[256,1024]{1,0:T(8,128)(2,1)}, bf16[256,1024]{1,0:T(8,128)(2,1)S(1)}, bf16[256,1024]{1,...) fusion(bf16[256,8192]{1,0:T(8,128)(2,1)} %param.3, ...), kind=kLoop, calls=%fused_computation | loop fusion | bytes 8388640 | tf_op jit(solution)/shard_map/dynamic_slice | solution.py:477
  3.9 3.0 %collective-permute-start.1 = (bf16[256,1024]{1,0:T(8,128)(2,1)}, bf16[256,1024]{1,0:T(8,128)(2,1)S(1)}, u32[]{:S(2)}, u32[]{:S(2)}) collective-permute-start(bf16[256,1024]{1,0:T(8,128)(2,1)} %get-tuple-element.56), channel_id=1, source_target_pairs={{0,2},{1,3},{2,0},{3,1},{4,6},{5,7},{6,4},{7,5},{8,10},{9,11},{10,... | collective-permute-start | bytes 1572872 | tf_op jit(solution)/shard_map/ppermute | solution.py:35
  7.6 14.2 %collective-permute-done.4.refs_2_ = bf16[64,1024]{1,0:T(8,128)(2,1)S(1)} collective-permute-done((bf16[64,1024]{1,0:T(8,128)(2,1)S(1)}, bf16[64,1024]{1,0:T(8,128)(2,1)S(1)}, u32[]{:S(2)}, u32[]{:S(2)}) %collective-permute-start.4) | collective-permute-done | bytes 131104 | tf_op jit(solution)/shard_map/ppermute | solution.py:35
  21.8 1.8 collective-permute-start.6
  23.6 3.1 %collective-permute-done.6.refs_4_ = bf16[64,1024]{1,0:T(8,128)(2,1)S(1)} collective-permute-done((bf16[64,1024]{1,0:T(8,128)(2,1)S(1)}, bf16[64,1024]{1,0:T(8,128)(2,1)S(1)}, u32[]{:S(2)}, u32[]{:S(2)}) %collective-permute-start.6) | collective-permute-done | bytes 131104 | tf_op jit(solution)/shard_map/ppermute | solution.py:35
  26.7 2.8 %collective-permute-start.7 = (bf16[64,1024]{1,0:T(8,128)(2,1)S(1)}, bf16[64,1024]{1,0:T(8,128)(2,1)S(1)}, u32[]{:S(2)}, u32[]{:S(2)}) collective-permute-start(bf16[64,1024]{1,0:T(8,128)(2,1)S(1)} %collective-permute-done.4.refs_2_), channel_id=1, source_target_pairs={{0,12},{4,8},{8,4},{12,0},{16,28},{20,24},{24,20},{28,16},{1,13},{... | collective-permute-start | bytes 393224 | tf_op jit(solution)/shard_map/ppermute | solution.py:35
  29.5 3.1 %collective-permute-done.7.refs_5_ = bf16[64,1024]{1,0:T(8,128)(2,1)S(1)} collective-permute-done((bf16[64,1024]{1,0:T(8,128)(2,1)S(1)}, bf16[64,1024]{1,0:T(8,128)(2,1)S(1)}, u32[]{:S(2)}, u32[]{:S(2)}) %collective-permute-start.7) | collective-permute-done | bytes 131104 | tf_op jit(solution)/shard_map/ppermute | solution.py:35
  34.5 3.2 %collective-permute-done.5.refs_3_ = bf16[64,1024]{1,0:T(8,128)(2,1)S(1)} collective-permute-done((bf16[64,1024]{1,0:T(8,128)(2,1)S(1)}, bf16[64,1024]{1,0:T(8,128)(2,1)S(1)}, u32[]{:S(2)}, u32[]{:S(2)}) %collective-permute-start.5) | collective-permute-done | bytes 131104 | tf_op jit(solution)/shard_map/ppermute | solution.py:35
  38.7 2.3 %begin.1 = (f32[1024,1024]{1,0:T(8,128)S(1)}, f32[1024,1024]{1,0:T(8,128)S(1)}, f32[1024,1024]{1,0:T(8,128)S(1)}) custom-call(bf16[256,1024]{1,0:T(8,128)(2,1)S(1)} %copy-done, bf16[256,1024]{1,0:T(8,128)(2,1)S(1)} %collective-permute-done.3.refs_1_, bf16[256,1024]{1,0:T(8,128)(2,1)S(1)} %get-tuple-element.57.refs_2_.refs_0_, ...), custom_call_target="tpu_custom_call" | custom-call | tf_op jit(solution)/shard_map/begin/pallas_call | solution.py:215
  40.9 1.8 collective-permute-start.23
  42.8 6.2 %out_factor.1 = (bf16[1024,1024]{1,0:T(8,128)(2,1)S(1)}, bf16[3,1024,1024]{2,1,0:T(8,128)(2,1)S(1)}, f32[8,128]{1,0:T(8,128)S(1)}) custom-call(bf16[256,1024]{1,0:T(8,128)(2,1)S(1)} %copy-done, bf16[256,1024]{1,0:T(8,128)(2,1)S(1)} %collective-permute-done.3.refs_1_, bf16[64,1024]{1,0:T(8,128)(2,1)S(1)} %collective-permute-done.4.refs_2_, ...), custom_call_target="tpu_custom_call" | custom-call | tf_op jit(solution)/shard_map/out_factor/pallas_call | solution.py:188
  49.0 9.0 %out_spread.1 = (bf16[1024,1024]{1,0:T(8,128)(2,1)S(1)}, bf16[1024,1024]{1,0:T(8,128)(2,1)S(1)}, bf16[1024,512]{1,0:T(8,128)(2,1)S(1)}, bf16[1024,512]{1,0:T(8,128)(2,1)S(1)}) custom-call(bf16[1024,1024]{1,0:T(8,128)(2,1)S(1)} %get-tuple-element.29.given, bf16[3,1024,1024]{2,1,0:T(8,128)(2,1)S(1)} %get-tuple-element.30.powers, ...), custom_call_target="tpu_custom_call" | custom-call | tf_op jit(solution)/shard_map/out_spread/pallas_call | solution.py:227
  58.0 11.3 %shard_map.37 = (bf16[8192,1024]{1,0:T(8,128)(2,1)}, bf16[1024,512]{1,0:T(8,128)(2,1)S(1)}, bf16[768,512]{1,0:T(8,128)(2,1)S(1)}, bf16[256,512]{1,0:T(8,128)(2,1)S(1)}) custom-call(f32[64]{0:T(128)S(1)} %copy-done.1, bf16[256,1024]{1,0:T(8,128)(2,1)S(1)} %get-tuple-element.57.refs_2_.refs_0_, bf16[256,1024]{1,0:T(8,128)(2,1)S(1)} %collective-permute-done.refs_3_.refs_1_, ...), custom_call_target="tpu_custom_call" | custom-call | tf_op jit(solution)/shard_map/pallas_call | solution.py:399
  71.7 11.4 %collective-permute-done.24.refs_3_ = bf16[256,1024]{1,0:T(8,128)(2,1)S(1)} collective-permute-done((bf16[256,1024]{1,0:T(8,128)(2,1)S(1)}, bf16[256,1024]{1,0:T(8,128)(2,1)S(1)}, u32[]{:S(2)}, u32[]{:S(2)}) %collective-permute-start.24) | collective-permute-done | bytes 524320 | tf_op jit(solution)/shard_map/ppermute | solution.py:35
  83.1 16.9 %shard_map.38 = (bf16[8192,1024]{1,0:T(8,128)(2,1)}, bf16[1024,1024]{1,0:T(8,128)(2,1)S(1)}) custom-call(f32[64]{0:T(128)S(1)} %copy-done.1, bf16[256,1024]{1,0:T(8,128)(2,1)S(1)} %get-tuple-element.55.refs_4_.refs_0_, bf16[256,1024]{1,0:T(8,128)(2,1)S(1)} %collective-permute-done.12.refs_5_.refs_1_, ...), custom_call_target="tpu_custom_call", output_to_operand_aliasing={{0}: (9, {})} | custom-call | tf_op jit(solution)/shard_map/pallas_call | solution.py:399
  101.1 4.5 %collective-permute-done.22.refs_3_ = bf16[256,1024]{1,0:T(8,128)(2,1)S(1)} collective-permute-done((bf16[256,1024]{1,0:T(8,128)(2,1)S(1)}, bf16[256,1024]{1,0:T(8,128)(2,1)S(1)}, u32[]{:S(2)}, u32[]{:S(2)}) %collective-permute-start.22) | collective-permute-done | bytes 524320 | tf_op jit(solution)/shard_map/ppermute | solution.py:35
  105.6 17.3 %shard_map.39 = (bf16[8192,1024]{1,0:T(8,128)(2,1)}, bf16[1024,1024]{1,0:T(8,128)(2,1)S(1)}) custom-call(f32[64]{0:T(128)S(1)} %copy-done.1, bf16[256,1024]{1,0:T(8,128)(2,1)S(1)} %get-tuple-element.58.refs_0_, bf16[256,1024]{1,0:T(8,128)(2,1)S(1)} %collective-permute-done.20.refs_1_, ...), custom_call_target="tpu_custom_call", output_to_operand_aliasing={{0}: (9, {})} | custom-call | tf_op jit(solution)/shard_map/pallas_call | solution.py:399
  125.6 2.4 %collective-permute-done.18.refs_1_ = bf16[256,1024]{1,0:T(8,128)(2,1)S(1)} collective-permute-done((bf16[256,1024]{1,0:T(8,128)(2,1)S(1)}, bf16[256,1024]{1,0:T(8,128)(2,1)S(1)}, u32[]{:S(2)}, u32[]{:S(2)}) %collective-permute-start.18) | collective-permute-done | bytes 524320 | tf_op jit(solution)/shard_map/ppermute | solution.py:35
  128.0 9.2 %collective-permute-done.19.refs_2_ = bf16[256,1024]{1,0:T(8,128)(2,1)S(1)} collective-permute-done((bf16[256,1024]{1,0:T(8,128)(2,1)S(1)}, bf16[256,1024]{1,0:T(8,128)(2,1)S(1)}, u32[]{:S(2)}, u32[]{:S(2)}) %collective-permute-start.19) | collective-permute-done | bytes 524320 | tf_op jit(solution)/shard_map/ppermute | solution.py:35
  137.1 5.2 %shard_map.40 = (bf16[8192,1024]{1,0:T(8,128)(2,1)}, f32[1024,1024]{1,0:T(8,128)S(1)}, f32[1024,1024]{1,0:T(8,128)S(1)}) custom-call(bf16[256,1024]{1,0:T(8,128)(2,1)S(1)} %get-tuple-element.53.refs_0_, bf16[256,1024]{1,0:T(8,128)(2,1)S(1)} %collective-permute-done.18.refs_1_, ...), custom_call_target="tpu_custom_call", output_to_operand_aliasing={{0}: (7, {})} | custom-call | tf_op jit(solution)/shard_map/pallas_call | solution.py:399
  142.4 6.6 %collective-permute-done.17.refs_0_ = bf16[256,1024]{1,0:T(8,128)(2,1)S(1)} collective-permute-done((bf16[256,1024]{1,0:T(8,128)(2,1)S(1)}, bf16[256,1024]{1,0:T(8,128)(2,1)S(1)}, u32[]{:S(2)}, u32[]{:S(2)}) %collective-permute-start.17) | collective-permute-done | bytes 524320 | tf_op jit(solution)/shard_map/ppermute | solution.py:35
  149.0 13.2 %shard_map.41 = (bf16[8192,1024]{1,0:T(8,128)(2,1)}, bf16[1024,1024]{1,0:T(8,128)(2,1)S(1)}) custom-call(f32[64]{0:T(128)S(1)} %copy-done.1, bf16[256,1024]{1,0:T(8,128)(2,1)S(1)} %collective-permute-done.17.refs_0_, bf16[1024,1024]{1,0:T(8,128)(2,1)S(1)} %get-tuple-element.37.refs_4_.refs_3_.refs_1_, ...), custom_call_target="tpu_custom_call", output_to_operand_aliasing={{0}: (7, {})} | custom-call | tf_op jit(solution)/shard_map/pallas_call | solution.py:399
  162.7 19.5 %collective-permute-done.15.refs_0_ = bf16[768,512]{1,0:T(8,128)(2,1)S(1)} collective-permute-done((bf16[768,512]{1,0:T(8,128)(2,1)S(1)}, bf16[768,512]{1,0:T(8,128)(2,1)S(1)}, u32[]{:S(2)}, u32[]{:S(2)}) %collective-permute-start.15) | collective-permute-done | bytes 786464 | tf_op jit(solution)/shard_map/ppermute | solution.py:35
  182.6 8.4 %collective-permute-done.13.refs_1_ = bf16[256,512]{1,0:T(8,128)(2,1)S(1)} collective-permute-done((bf16[256,512]{1,0:T(8,128)(2,1)S(1)}, bf16[256,512]{1,0:T(8,128)(2,1)S(1)}, u32[]{:S(2)}, u32[]{:S(2)}) %collective-permute-start.13) | collective-permute-done | bytes 262176 | tf_op jit(solution)/shard_map/ppermute | solution.py:35
  (58 shorter events, 15.2 us)
Async XLA Ops:
  3.9 19.7 %collective-permute-start.1 = (bf16[256,1024]{1,0:T(8,128)(2,1)}, bf16[256,1024]{1,0:T(8,128)(2,1)S(1)}, u32[]{:S(2)}, u32[]{:S(2)}) collective-permute-start(bf16[256,1024]{1,0:T(8,128)(2,1)} %get-tuple-element.56), channel_id=1, source_target_pairs={{0,2},{1,3},{2,0},{3,1},{4,6},{5,7},{6,4},{7,5},{8,10},{9,11},{10,... | collective-permute-start | bytes 1572872 | tf_op jit(solution)/shard_map/ppermute | solution.py:35
  6.9 14.9 %collective-permute-start.4 = (bf16[64,1024]{1,0:T(8,128)(2,1)S(1)}, bf16[64,1024]{1,0:T(8,128)(2,1)S(1)}, u32[]{:S(2)}, u32[]{:S(2)}) collective-permute-start(bf16[64,1024]{1,0:T(8,128)(2,1)S(1)} %constant_dynamic-slice_fusion.6), channel_id=1, source_target_pairs={{0,2},{1,3},{2,0},{3,1},{4,6},{5,7},{6,4},{7,5},{8,10},{9,11},{10,... | collective-permute-start | bytes 393224 | tf_op jit(solution)/shard_map/ppermute | solution.py:35
  6.9 30.7 %collective-permute-start = (bf16[256,1024]{1,0:T(8,128)(2,1)S(1)}, bf16[256,1024]{1,0:T(8,128)(2,1)S(1)}, u32[]{:S(2)}, u32[]{:S(2)}) collective-permute-start(bf16[256,1024]{1,0:T(8,128)(2,1)S(1)} %get-tuple-element.57.refs_2_.refs_0_), channel_id=1, source_target_pairs={{0,1},{1,0},{2,3},{3,2},{4,5},{5,4},{6,7},{7,6},{8,9},{9,8},{10,11... | collective-permute-start | bytes 1572872 | tf_op jit(solution)/shard_map/ppermute | solution.py:35
  7.0 31.1 %collective-permute-start.12 = (bf16[256,1024]{1,0:T(8,128)(2,1)}, bf16[256,1024]{1,0:T(8,128)(2,1)S(1)}, u32[]{:S(2)}, u32[]{:S(2)}) collective-permute-start(bf16[256,1024]{1,0:T(8,128)(2,1)} %get-tuple-element.54), channel_id=1, source_target_pairs={{0,1},{1,0},{2,3},{3,2},{4,5},{5,4},{6,7},{7,6},{8,9},{9,8},{10,11... | collective-permute-start | bytes 1572872 | tf_op jit(solution)/shard_map/ppermute | solution.py:35
  7.5 30.7 %collective-permute-start.3 = (bf16[256,1024]{1,0:T(8,128)(2,1)S(1)}, bf16[256,1024]{1,0:T(8,128)(2,1)S(1)}, u32[]{:S(2)}, u32[]{:S(2)}) collective-permute-start(bf16[256,1024]{1,0:T(8,128)(2,1)S(1)} %copy-done), channel_id=1, source_target_pairs={{0,1},{1,0},{2,3},{3,2},{4,5},{5,4},{6,7},{7,6},{8,9},{9,8},{10,11... | collective-permute-start | bytes 1572872 | tf_op jit(solution)/shard_map/ppermute | solution.py:35
  21.8 5.0 %collective-permute-start.6 = (bf16[64,1024]{1,0:T(8,128)(2,1)S(1)}, bf16[64,1024]{1,0:T(8,128)(2,1)S(1)}, u32[]{:S(2)}, u32[]{:S(2)}) collective-permute-start(bf16[64,1024]{1,0:T(8,128)(2,1)S(1)} %collective-permute-done.4.refs_2_), channel_id=1, source_target_pairs={{0,8},{4,12},{8,0},{12,4},{16,24},{20,28},{24,16},{28,20},{1,9},{5... | collective-permute-start | bytes 393224 | tf_op jit(solution)/shard_map/ppermute | solution.py:35
  23.6 34.4 %collective-permute-start.2 = (bf16[256,1024]{1,0:T(8,128)(2,1)S(1)}, bf16[256,1024]{1,0:T(8,128)(2,1)S(1)}, u32[]{:S(2)}, u32[]{:S(2)}) collective-permute-start(bf16[256,1024]{1,0:T(8,128)(2,1)S(1)} %collective-permute-done.1.refs_2_), channel_id=1, source_target_pairs={{0,1},{1,0},{2,3},{3,2},{4,5},{5,4},{6,7},{7,6},{8,9},{9,8},{10,11... | collective-permute-start | bytes 1572872 | tf_op jit(solution)/shard_map/ppermute | solution.py:35
  26.7 5.9 %collective-permute-start.7 = (bf16[64,1024]{1,0:T(8,128)(2,1)S(1)}, bf16[64,1024]{1,0:T(8,128)(2,1)S(1)}, u32[]{:S(2)}, u32[]{:S(2)}) collective-permute-start(bf16[64,1024]{1,0:T(8,128)(2,1)S(1)} %collective-permute-done.4.refs_2_), channel_id=1, source_target_pairs={{0,12},{4,8},{8,4},{12,0},{16,28},{20,24},{24,20},{28,16},{1,13},{... | collective-permute-start | bytes 393224 | tf_op jit(solution)/shard_map/ppermute | solution.py:35
  32.7 5.0 %collective-permute-start.5 = (bf16[64,1024]{1,0:T(8,128)(2,1)S(1)}, bf16[64,1024]{1,0:T(8,128)(2,1)S(1)}, u32[]{:S(2)}, u32[]{:S(2)}) collective-permute-start(bf16[64,1024]{1,0:T(8,128)(2,1)S(1)} %collective-permute-done.4.refs_2_), channel_id=1, source_target_pairs={{0,4},{4,0},{8,12},{12,8},{16,20},{20,16},{24,28},{28,24},{1,5},{5... | collective-permute-start | bytes 393224 | tf_op jit(solution)/shard_map/ppermute | solution.py:35
  37.6 5.2 %collective-permute-start.10 = (bf16[64,1024]{1,0:T(8,128)(2,1)S(1)}, bf16[64,1024]{1,0:T(8,128)(2,1)S(1)}, u32[]{:S(2)}, u32[]{:S(2)}) collective-permute-start(bf16[64,1024]{1,0:T(8,128)(2,1)S(1)} %collective-permute-done.6.refs_4_), channel_id=1, source_target_pairs={{0,1},{1,0},{2,3},{3,2},{4,5},{5,4},{6,7},{7,6},{8,9},{9,8},{10,11... | collective-permute-start | bytes 393224 | tf_op jit(solution)/shard_map/ppermute | solution.py:35
  40.9 30.7 %collective-permute-start.23 = (bf16[256,1024]{1,0:T(8,128)(2,1)S(1)}, bf16[256,1024]{1,0:T(8,128)(2,1)S(1)}, u32[]{:S(2)}, u32[]{:S(2)}) collective-permute-start(bf16[256,1024]{1,0:T(8,128)(2,1)S(1)} %get-tuple-element.55.refs_4_.refs_0_), channel_id=1, source_target_pairs={{0,2},{1,3},{2,0},{3,1},{4,6},{5,7},{6,4},{7,5},{8,10},{9,11},{10,... | collective-permute-start | bytes 1572872 | tf_op jit(solution)/shard_map/ppermute | solution.py:35
  69.4 36.2 %collective-permute-start.25 = (bf16[1024,512]{1,0:T(8,128)(2,1)S(1)}, bf16[1024,512]{1,0:T(8,128)(2,1)S(1)}, u32[]{:S(2)}, u32[]{:S(2)}) collective-permute-start(bf16[1024,512]{1,0:T(8,128)(2,1)S(1)} %get-tuple-element.40.refs_7_), channel_id=1, source_target_pairs={{0,1},{1,0},{2,3},{3,2},{4,5},{5,4},{6,7},{7,6},{8,9},{9,8},{10,11... | collective-permute-start | bytes 3145736 | tf_op jit(solution)/shard_map/ppermute | solution.py:35
  69.4 13.7 %collective-permute-start.24 = (bf16[256,1024]{1,0:T(8,128)(2,1)S(1)}, bf16[256,1024]{1,0:T(8,128)(2,1)S(1)}, u32[]{:S(2)}, u32[]{:S(2)}) collective-permute-start(bf16[256,1024]{1,0:T(8,128)(2,1)S(1)} %copy-done.4), channel_id=1, source_target_pairs={{0,3},{1,2},{2,1},{3,0},{4,7},{5,6},{6,5},{7,4},{8,11},{9,10},{10,... | collective-permute-start | bytes 1572872 | tf_op jit(solution)/shard_map/ppermute | solution.py:35
  69.8 31.3 %collective-permute-start.20 = (bf16[256,1024]{1,0:T(8,128)(2,1)S(1)}, bf16[256,1024]{1,0:T(8,128)(2,1)S(1)}, u32[]{:S(2)}, u32[]{:S(2)}) collective-permute-start(bf16[256,1024]{1,0:T(8,128)(2,1)S(1)} %copy-done.3), channel_id=1, source_target_pairs={{0,1},{1,0},{2,3},{3,2},{4,5},{5,4},{6,7},{7,6},{8,9},{9,8},{10,11... | collective-permute-start | bytes 1572872 | tf_op jit(solution)/shard_map/ppermute | solution.py:35
  70.0 31.1 %collective-permute-start.21 = (bf16[256,1024]{1,0:T(8,128)(2,1)S(1)}, bf16[256,1024]{1,0:T(8,128)(2,1)S(1)}, u32[]{:S(2)}, u32[]{:S(2)}) collective-permute-start(bf16[256,1024]{1,0:T(8,128)(2,1)S(1)} %get-tuple-element.58.refs_0_), channel_id=1, source_target_pairs={{0,2},{1,3},{2,0},{3,1},{4,6},{5,7},{6,4},{7,5},{8,10},{9,11},{10,... | collective-permute-start | bytes 1572872 | tf_op jit(solution)/shard_map/ppermute | solution.py:35
  71.7 33.9 %collective-permute-start.22 = (bf16[256,1024]{1,0:T(8,128)(2,1)S(1)}, bf16[256,1024]{1,0:T(8,128)(2,1)S(1)}, u32[]{:S(2)}, u32[]{:S(2)}) collective-permute-start(bf16[256,1024]{1,0:T(8,128)(2,1)S(1)} %copy-done.3), channel_id=1, source_target_pairs={{0,3},{1,2},{2,1},{3,0},{4,7},{5,6},{6,5},{7,4},{8,11},{9,10},{10,... | collective-permute-start | bytes 1572872 | tf_op jit(solution)/shard_map/ppermute | solution.py:35
  100.0 37.1 %collective-permute-start.26 = (bf16[1024,1024]{1,0:T(8,128)(2,1)S(1)}, bf16[1024,1024]{1,0:T(8,128)(2,1)S(1)}, u32[]{:S(2)}, u32[]{:S(2)}) collective-permute-start(bf16[1024,1024]{1,0:T(8,128)(2,1)S(1)} %get-tuple-element.42.refs_6_), channel_id=1, source_target_pairs={{0,1},{1,0},{2,3},{3,2},{4,5},{5,4},{6,7},{7,6},{8,9},{9,8},{10,11... | collective-permute-start | bytes 6291464 | tf_op jit(solution)/shard_map/ppermute | solution.py:35
  122.9 26.0 %collective-permute-start.27 = (bf16[1024,1024]{1,0:T(8,128)(2,1)S(1)}, bf16[1024,1024]{1,0:T(8,128)(2,1)S(1)}, u32[]{:S(2)}, u32[]{:S(2)}) collective-permute-start(bf16[1024,1024]{1,0:T(8,128)(2,1)S(1)} %get-tuple-element.44.refs_5_), channel_id=1, source_target_pairs={{0,1},{1,0},{2,3},{3,2},{4,5},{5,4},{6,7},{7,6},{8,9},{9,8},{10,11... | collective-permute-start | bytes 6291464 | tf_op jit(solution)/shard_map/ppermute | solution.py:35
  123.5 13.6 %collective-permute-start.19 = (bf16[256,1024]{1,0:T(8,128)(2,1)S(1)}, bf16[256,1024]{1,0:T(8,128)(2,1)S(1)}, u32[]{:S(2)}, u32[]{:S(2)}) collective-permute-start(bf16[256,1024]{1,0:T(8,128)(2,1)S(1)} %copy-done.2), channel_id=1, source_target_pairs={{0,3},{1,2},{2,1},{3,0},{4,7},{5,6},{6,5},{7,4},{8,11},{9,10},{10,... | collective-permute-start | bytes 1572872 | tf_op jit(solution)/shard_map/ppermute | solution.py:35
  123.8 25.1 %collective-permute-start.17 = (bf16[256,1024]{1,0:T(8,128)(2,1)S(1)}, bf16[256,1024]{1,0:T(8,128)(2,1)S(1)}, u32[]{:S(2)}, u32[]{:S(2)}) collective-permute-start(bf16[256,1024]{1,0:T(8,128)(2,1)S(1)} %get-tuple-element.53.refs_0_), channel_id=1, source_target_pairs={{0,2},{1,3},{2,0},{3,1},{4,6},{5,7},{6,4},{7,5},{8,10},{9,11},{10,... | collective-permute-start | bytes 1572872 | tf_op jit(solution)/shard_map/ppermute | solution.py:35
  162.2 30.4 %collective-permute-start.28 = (bf16[1024,1024]{1,0:T(8,128)(2,1)S(1)}, bf16[1024,1024]{1,0:T(8,128)(2,1)S(1)}, u32[]{:S(2)}, u32[]{:S(2)}) collective-permute-start(bf16[1024,1024]{1,0:T(8,128)(2,1)S(1)} %get-tuple-element.49.refs_1_), channel_id=1, source_target_pairs={{0,1},{1,0},{2,3},{3,2},{4,5},{5,4},{6,7},{7,6},{8,9},{9,8},{10,11... | collective-permute-start | bytes 6291464 | tf_op jit(solution)/shard_map/ppermute | solution.py:35
  162.3 19.9 %collective-permute-start.15 = (bf16[768,512]{1,0:T(8,128)(2,1)S(1)}, bf16[768,512]{1,0:T(8,128)(2,1)S(1)}, u32[]{:S(2)}, u32[]{:S(2)}) collective-permute-start(bf16[768,512]{1,0:T(8,128)(2,1)S(1)} %get-tuple-element.36), channel_id=1, source_target_pairs={{0,2},{1,3},{2,0},{3,1},{4,6},{5,7},{6,4},{7,5},{8,10},{9,11},{10,... | collective-permute-start | bytes 2359304 | tf_op jit(solution)/shard_map/ppermute | solution.py:35
  182.2 11.7 %collective-permute-start.16 = (bf16[768,512]{1,0:T(8,128)(2,1)S(1)}, bf16[768,512]{1,0:T(8,128)(2,1)S(1)}, u32[]{:S(2)}, u32[]{:S(2)}) collective-permute-start(bf16[768,512]{1,0:T(8,128)(2,1)S(1)} %collective-permute-done.15.refs_0_), channel_id=1, source_target_pairs={{0,1},{1,0},{2,3},{3,2},{4,5},{5,4},{6,7},{7,6},{8,9},{9,8},{10,11... | collective-permute-start | bytes 2359304 | tf_op jit(solution)/shard_map/ppermute | solution.py:35
  182.2 8.7 %collective-permute-start.13 = (bf16[256,512]{1,0:T(8,128)(2,1)S(1)}, bf16[256,512]{1,0:T(8,128)(2,1)S(1)}, u32[]{:S(2)}, u32[]{:S(2)}) collective-permute-start(bf16[256,512]{1,0:T(8,128)(2,1)S(1)} %get-tuple-element.35), channel_id=1, source_target_pairs={{0,2},{1,3},{2,0},{3,1},{4,6},{5,7},{6,4},{7,5},{8,10},{9,11},{10,... | collective-permute-start | bytes 786440 | tf_op jit(solution)/shard_map/ppermute | solution.py:35
  (10 other events, 78.0 us)
